TPU v7x, 128 devices: a whole 4x4x4 slice. The times are simulated.
128 devices in a mesh: seq: 8 (over x, z_hi), role: 2 (over z_lo), exp: 8 (over y, core).
Axes of the slice: x: 4, y: 4, z: 4 (z_hi: 2, z_lo: 2; z = z_hi * 2 + z_lo), core: 2. Of those that a mesh axis runs over, the one named last changes fastest.
Arguments:
- tokens: bfloat16 [2, 65536, 768], P(None, ('seq', 'role', 'exp')), may hold values from -6 to 6
- expert_ids: int32 [2, 65536, 1], P(None, ('seq', 'role', 'exp')), may hold values from 0 to 127; in each aligned block of 512 rows (0 to 511, 512 to 1023, ..., all dimensions but the last counted through in order) at most 8 rows name the same one
- attn_qkv: bfloat16 [768, 2304], P(('seq', 'role')), may hold values from -0.21875 to 0.21875
- attn_out: bfloat16 [768, 768], P(('seq', 'role')), may hold values from -0.21875 to 0.21875
- norm_attn: float32 [768], replicated, may hold values from 0.1 to 1.9
- norm_ffn: float32 [768], replicated, may hold values from 0.1 to 1.9
- router: bfloat16 [768, 128], replicated, may hold values from -0.43164062 to 0.43164062
- expert_in: bfloat16 [128, 768, 3072], P(('seq', 'role', 'exp')), may hold values from -0.21875 to 0.21875
- expert_out: bfloat16 [128, 3072, 768], P(('seq', 'role', 'exp')), may hold values from -0.109375 to 0.109375
Outputs:
- layer_out: bfloat16 [2, 65536, 768], P(None, ('seq', 'role', 'exp'))
Inputs may be any that keep to these rules, and one draw needn't show every extreme that they name: `expert_ids`: in each micro-batch the 512 tokens of one device name any one expert at most 8 times.
All inputs are finite; a program needn't handle non-finite values.
Results may differ from a plain program's by a relative error of at most 0.0058.
Values may be sent and summed in bfloat16 or wider, within the bound.
No kernel may reach another device: no remote copies, remote signals or barrier semaphores. Data moves between devices by JAX's collectives and lax.ppermute only.
A program may use at most 128 MiB of HBM per device.

v0:
```python
import functools

import jax
import jax.numpy as jnp
from jax import lax
from jax.experimental import pallas as pl
from jax.experimental.pallas import tpu as pltpu
from jax.sharding import PartitionSpec as P

HEADS = 12
HALF = 384
SLOTS = 8
ALL = ("seq", "role", "exp")
F32 = jnp.float32
BF16 = jnp.bfloat16


def place(x, z, y, c):
    return x * 32 + z * 8 + y * 2 + c


def hop(d, phase):
    pairs = []
    for x in range(4):
        for z in range(4):
            for y in range(4):
                for c in range(2):
                    if (c == 0) == (phase == 0):
                        to = place((x + d) % 4, z, y, c)
                    else:
                        to = place(x, (z + d) % 4, y, c)
                    pairs.append((place(x, z, y, c), to))
    return pairs


def my_core():
    return lax.rem(lax.axis_index("exp"), 2)


def scale_rows(values, gain):
    floats = values.astype(F32)
    return floats * lax.rsqrt(jnp.mean(floats * floats, -1, keepdims=True) + 1e-06) * gain


def fetch(blocks, core, w, sem, wo=None, wo_sem=None):
    own, rest = blocks
    seq = lax.axis_index("seq")
    x = seq // 2
    z = lax.rem(seq, 2) * 2 + lax.axis_index("role")
    shift = (0, 3, 1, 2)
    copies, late = [], []
    for i in range(4):
        for j in range(4):
            source, at = (own, j * 48) if i == 0 else (rest, (i * 4 + j - 4) * 48)
            dx = jnp.where(core == 0, shift[j], shift[i])
            dz = jnp.where(core == 0, shift[i], shift[j])
            row = (lax.rem(x + dx, 4) * 4 + lax.rem(z + dz, 4)) * 48
            row = pl.multiple_of(row, 16)
            if w is not None:
                copies.append(
                    pltpu.make_async_copy(
                        source.at[pl.ds(at, 48), pl.ds(0, 3 * HALF)],
                        w.at[core, pl.ds(row, 48), :],
                        sem.at[i * 4 + j],
                    )
                )
            if wo is not None:
                late.append(
                    pltpu.make_async_copy(
                        source.at[pl.ds(at, 48), pl.ds(3 * HALF, HALF)],
                        wo.at[pl.ds(row, 48), pl.ds(pl.multiple_of(core * HALF, 128), HALF)],
                        wo_sem.at[i * 4 + j],
                    )
                )
    for copy in copies + late:
        copy.start()
    return copies, late


def wait_all(copies):
    for copy in copies:
        copy.wait()


def project(normed, weights, projected):
    projected[...] = jnp.dot(normed[...], weights[...], preferred_element_type=F32).astype(BF16)


def start_all(pairs, sems):
    copies = [
        pltpu.make_async_copy(source, target, sems.at[i]) for i, (source, target) in enumerate(pairs)
    ]
    for copy in copies:
        copy.start()
    return copies


def attend(projected, store):
    rows = projected.shape[0]
    block = 256
    low = lax.broadcasted_iota(jnp.int32, (block, 128), 1) < 64
    for pair in range(3):
        at = pair * 128
        k = projected[:, HALF + at : HALF + at + 128]
        v = projected[:, 2 * HALF + at : 2 * HALF + at + 128]
        values = jnp.concatenate([v, jnp.ones((rows, 128), BF16)], axis=1)
        for row in range(0, rows, block):
            q = projected[row : row + block, at : at + 128] * jnp.asarray(0.125, BF16)
            zero = jnp.zeros_like(q)
            outs = []
            for side in range(2):
                mine = jnp.where(low, q, zero) if side == 0 else jnp.where(low, zero, q)
                scores = lax.dot_general(
                    mine, k, (((1,), (1,)), ((), ())), preferred_element_type=F32
                )
                weight = jnp.exp(scores - jnp.max(scores, -1, keepdims=True)).astype(BF16)
                total = jnp.dot(weight, values, preferred_element_type=F32)
                outs.append(total[:, :128] / total[:, 128:])
            store(pair, row, jnp.where(low, outs[0], outs[1]).astype(BF16))


def context_kernel(
    x_ref, gain_ref, b0, b1, ctx_ref, normed_ref, x, gain, w, projected, sem, small
):
    core = my_core()
    loads = start_all([(x_ref.at[0], x), (gain_ref, gain)], small)
    copies, _ = fetch((b0, b1), core, w, sem)
    wait_all(loads)
    normed_ref[...] = scale_rows(x[...], gain[...]).astype(BF16)
    wait_all(copies)
    project(normed_ref, w.at[core], projected)

    def store(pair, row, context):
        ctx_ref[row : row + context.shape[0], pair * 128 : pair * 128 + 128] = context

    attend(projected, store)


def finish(
    x, ctx, wo, gain, router, ids, att_ref, out_ref, aux_ref, normed, sent, att, aux, sems
):
    rows, experts = x.shape[0], router.shape[1]
    block = 256
    for row in range(0, rows, block):
        mine = slice(row, row + block)
        both = jnp.concatenate([ctx[0, mine], ctx[1, mine]], axis=1)
        mixed = jnp.dot(both, wo[...], preferred_element_type=F32)
        attended = (x[mine].astype(F32) + mixed).astype(BF16)
        att[mine] = attended
        normed[mine] = scale_rows(attended, gain[...]).astype(BF16)
    copies = [pltpu.make_async_copy(att, att_ref, sems.at[4])]
    copies[0].start()
    ids_row = ids[...]
    logits = lax.dot_general(
        router[...], normed[...], (((0,), (1,)), ((), ())), preferred_element_type=F32
    )
    i0 = lax.broadcasted_iota(jnp.int32, (rows, rows), 0)
    i1 = lax.broadcasted_iota(jnp.int32, (rows, rows), 1)
    picked = ids_row == lax.broadcasted_iota(jnp.int32, (experts, rows), 0)
    gate = jax.nn.sigmoid(jnp.sum(jnp.where(picked, logits, 0.0), 0, keepdims=True))
    running = jnp.dot(
        picked.astype(F32).astype(BF16),
        (i0 <= i1).astype(F32).astype(BF16),
        preferred_element_type=F32,
    )
    rank = jnp.sum(jnp.where(picked, running, 0.0), 0, keepdims=True)
    position = ids_row * SLOTS + rank.astype(jnp.int32) - 1
    aux_row = lax.broadcasted_iota(jnp.int32, (128, rows), 0)
    aux[...] = jnp.where(aux_row == 0, gate, position.astype(F32)).T
    copies.append(pltpu.make_async_copy(aux, aux_ref, sems.at[5]))
    copies[1].start()
    for slot in range(0, experts * SLOTS, block):
        number = lax.broadcasted_iota(jnp.int32, (block, rows), 0) + slot
        spread = (number == position).astype(F32).astype(BF16)
        some = pl.ds(slot // SLOTS, block // SLOTS)
        sent[some] = (
            jnp.dot(spread, normed[...], preferred_element_type=F32)
            .astype(BF16)
            .reshape(block // SLOTS, SLOTS, normed.shape[1])
        )
        copy = pltpu.make_async_copy(sent.at[some], out_ref.at[some], sems.at[slot // block])
        copy.start()
        copies.append(copy)
    wait_all(copies)


def second_half_kernel(
    x_ref, normed_ref, m0, m1, o0, o1, ctx_ref, gain_ref, router_ref, row_ref,
    att_ref, out_ref, aux_ref,
    x, gain, router, ids, w, wo, ctx, projected, normed, sent, att, aux, sems, small,
):
    core = my_core()
    qkv, late = fetch((o0, o1), 1 - core, w, sems.at[0], wo, sems.at[1])
    _, later = fetch((m0, m1), core, None, None, wo, sems.at[2])
    loads = start_all(
        [(x_ref.at[0], x), (gain_ref, gain), (router_ref, router), (row_ref.at[0], ids)], small
    )
    ctx[core] = ctx_ref[...]
    wait_all(qkv)
    project(normed_ref, w.at[1 - core], projected)

    def store(pair, row, context):
        ctx[1 - core, row : row + context.shape[0], pair * 128 : pair * 128 + 128] = context

    attend(projected, store)
    wait_all(late + later + loads)
    finish(x, ctx, wo, gain, router, ids, att_ref, out_ref, aux_ref, normed, sent, att, aux, small)


def whole_kernel(
    x_ref, gain1_ref, m0, m1, o0, o1, gain_ref, router_ref, row_ref,
    att_ref, out_ref, aux_ref,
    gain1, x, gain, router, ids, w, wo, ctx, projected, normed, sent, att, aux, sems, small,
):
    core = my_core()
    first = start_all([(x_ref.at[1], x), (gain1_ref, gain1)], small)
    qkv, late = fetch((m0, m1), core, w, sems.at[0], wo, sems.at[1])
    qkv2, late2 = fetch((o0, o1), 1 - core, w, sems.at[2], wo, sems.at[3])
    loads = start_all(
        [(gain_ref, gain), (router_ref, router), (row_ref.at[1], ids)], small.at[pl.ds(2, 3)]
    )
    wait_all(first)
    normed[...] = scale_rows(x[...], gain1[...]).astype(BF16)
    wait_all(qkv + qkv2)

    def step(side, carry):
        def store(pair, row, context):
            ctx[side, row : row + context.shape[0], pair * 128 : pair * 128 + 128] = context

        project(normed, w.at[side], projected)
        attend(projected, store)
        return carry

    lax.fori_loop(0, 2, step, 0)
    wait_all(late + late2 + loads)
    finish(x, ctx, wo, gain, router, ids, att_ref, out_ref, aux_ref, normed, sent, att, aux, small)


def expert_kernel(x_ref, in_ref, out_ref, y_ref, total, hidden):
    step = pl.program_id(0)
    slots, width = total.shape
    block = 256
    x = x_ref.reshape(slots, width)

    @pl.when(step == 0)
    def _():
        total[...] = jnp.zeros_like(total)

    for at in range(0, slots, block):
        first = jnp.dot(x[at : at + block], in_ref[0], preferred_element_type=F32)
        hidden[at : at + block] = jnp.maximum(first, 0.0).astype(BF16)
    for at in range(0, slots, block):
        total[at : at + block] += jnp.dot(
            hidden[at : at + block], out_ref[0], preferred_element_type=F32
        )

    @pl.when(step == pl.num_programs(0) - 1)
    def _():
        y_ref[...] = total[...].astype(BF16).reshape(y_ref.shape)


def combine_kernel(batch, att_ref, aux_ref, back_ref, out_ref, att, aux, done, sems):
    rows, width = att.shape
    slots = back_ref.shape[0] * SLOTS
    block = 128
    back = back_ref.reshape(slots, width)
    loads = start_all([(aux_ref, aux), (att_ref, att)], sems.at[pl.ds(4, 2)])
    loads[0].wait()
    copies = []
    for row in range(0, rows, block):
        mine = pl.ds(row, block)
        gate = aux[mine, 0:1]
        position = aux[mine, 1:2].astype(jnp.int32)
        pick = lax.broadcasted_iota(jnp.int32, (block, slots), 1) == position
        result = jnp.dot(pick.astype(F32).astype(BF16), back[...], preferred_element_type=F32)
        if row == 0:
            loads[1].wait()
        done[mine] = (att[mine].astype(F32) + gate * result).astype(BF16)
        copy = pltpu.make_async_copy(done.at[mine], out_ref.at[batch, mine], sems.at[row // block])
        copy.start()
        copies.append(copy)
    wait_all(copies)


def combine_after_kernel(batch, att_ref, aux_ref, back_ref, held_ref, out_ref, *scratch):
    del held_ref
    combine_kernel(batch, att_ref, aux_ref, back_ref, out_ref, *scratch)


def limit(kibibytes):
    return pltpu.CompilerParams(vmem_limit_bytes=kibibytes << 10)


def full(shape):
    return pl.BlockSpec(shape, lambda i: (0,) * len(shape))


def body(
    tokens, expert_ids, attn_qkv, attn_out, norm_attn, norm_ffn, router, expert_in, expert_out
):
    batches, rows, width = tokens.shape
    experts = router.shape[1]
    slots = experts * SLOTS
    core = my_core()
    halves = [
        jnp.concatenate(
            [attn_qkv[:, at + side * HALF : at + side * HALF + HALF] for at in (0, width, 2 * width)]
            + [attn_out[:, side * HALF : side * HALF + HALF]],
            axis=1,
        )
        for side in range(2)
    ]
    piece = jnp.where(core == 0, halves[0], halves[1])
    swap = [(i, i ^ 1) for i in range(128)]
    steps = (1, -1, 2)
    own = jnp.concatenate([piece] + [lax.ppermute(piece, ALL, hop(d, 0)) for d in steps], axis=0)
    rest = jnp.concatenate([lax.ppermute(own, ALL, hop(d, 1)) for d in steps], axis=0)
    mine = [own, rest]
    other = [lax.ppermute(part, ALL, swap) for part in mine]
    mine = [pltpu.with_memory_space_constraint(part, pltpu.VMEM) for part in mine]
    other = [pltpu.with_memory_space_constraint(part, pltpu.VMEM) for part in other]

    ids_row = expert_ids.reshape(batches, 1, rows)

    any_spec = pl.BlockSpec(memory_space=pltpu.HBM)
    whole = pl.BlockSpec(memory_space=pltpu.VMEM)

    def near(value):
        return pltpu.with_memory_space_constraint(value, pltpu.VMEM)

    def far(value):
        return pltpu.with_memory_space_constraint(value, pltpu.HBM)

    w_scratch = pltpu.VMEM((2, width, 3 * HALF), BF16)
    projected = pltpu.VMEM((rows, 3 * HALF), BF16)
    one = pltpu.VMEM((rows, width), BF16)
    gain_scratch = pltpu.VMEM((width,), F32)
    ctx_mine, normed = pl.pallas_call(
        context_kernel,
        out_shape=(
            jax.ShapeDtypeStruct((rows, HALF), BF16),
            jax.ShapeDtypeStruct((rows, width), BF16),
        ),
        in_specs=[any_spec] * 2 + [whole] * 2,
        out_specs=(whole, whole),
        scratch_shapes=[
            one,
            gain_scratch,
            w_scratch,
            projected,
            pltpu.SemaphoreType.DMA((16,)),
            pltpu.SemaphoreType.DMA((2,)),
        ],
        compiler_params=limit(47104),
        name="first_half",
    )(tokens, norm_attn, *mine)

    finish_out = (
        jax.ShapeDtypeStruct((rows, width), BF16),
        jax.ShapeDtypeStruct((experts, SLOTS, width), BF16),
        jax.ShapeDtypeStruct((rows, 128), F32),
    )
    finish_specs = (any_spec, any_spec, any_spec)
    scratch = [
        one,
        gain_scratch,
        pltpu.VMEM((width, experts), BF16),
        pltpu.VMEM((1, rows), jnp.int32),
        w_scratch,
        pltpu.VMEM((width, width), BF16),
        pltpu.VMEM((2, rows, HALF), BF16),
        projected,
        one,
        pltpu.VMEM((experts, SLOTS, width), BF16),
        one,
        pltpu.VMEM((rows, 128), F32),
        pltpu.SemaphoreType.DMA((4, 16)),
        pltpu.SemaphoreType.DMA((6,)),
    ]

    first = pl.pallas_call(
        second_half_kernel,
        out_shape=finish_out,
        in_specs=[any_spec] + [whole] * 6 + [any_spec] * 3,
        out_specs=finish_specs,
        scratch_shapes=scratch,
        compiler_params=limit(55900),
        name="second_half",
    )(tokens, near(normed), *mine, *other, near(ctx_mine), norm_ffn, router, ids_row)

    second = pl.pallas_call(
        whole_kernel,
        out_shape=finish_out,
        in_specs=[any_spec] * 2 + [whole] * 4 + [any_spec] * 3,
        out_specs=finish_specs,
        scratch_shapes=[gain_scratch] + scratch,
        compiler_params=limit(55500),
        name="whole",
    )(tokens, norm_attn, *mine, *other, norm_ffn, router, ids_row)

    def exchange(values):
        moved = lax.all_to_all(values, ALL, split_axis=0, concat_axis=0, tiled=True)
        return pltpu.with_memory_space_constraint(moved, pltpu.VMEM)

    hidden = expert_in.shape[2]
    chunk = 512
    def serve(values):
        return pl.pallas_call(
            expert_kernel,
            grid=(hidden // chunk,),
            out_shape=jax.ShapeDtypeStruct((experts, SLOTS, width), BF16),
            in_specs=[
                whole,
                pl.BlockSpec((1, width, chunk), lambda j: (0, 0, j)),
                pl.BlockSpec((1, chunk, width), lambda j: (0, j, 0)),
            ],
            out_specs=pl.BlockSpec((experts, SLOTS, width), lambda j: (0, 0, 0)),
            scratch_shapes=[pltpu.VMEM((slots, width), F32), pltpu.VMEM((slots, chunk), BF16)],
            compiler_params=limit(58300),
            name="expert",
        )(values, far(expert_in), far(expert_out))

    arrived = [exchange(first[1]), exchange(second[1])]
    back = [exchange(serve(values)) for values in arrived]

    out_shape = jax.ShapeDtypeStruct((batches, rows, width), BF16)
    combine_scratch = [
        one,
        pltpu.VMEM((rows, 128), F32),
        one,
        pltpu.SemaphoreType.DMA((6,)),
    ]
    held = pl.pallas_call(
        functools.partial(combine_kernel, 0),
        out_shape=out_shape,
        in_specs=[any_spec] * 2 + [whole],
        out_specs=any_spec,
        scratch_shapes=combine_scratch,
        compiler_params=limit(58300),
        name="combine0",
    )(first[0], first[2], back[0])
    return pl.pallas_call(
        functools.partial(combine_after_kernel, 1),
        out_shape=out_shape,
        in_specs=[any_spec] * 2 + [whole, any_spec],
        out_specs=any_spec,
        scratch_shapes=combine_scratch,
        input_output_aliases={3: 0},
        compiler_params=limit(58300),
        name="combine1",
    )(second[0], second[2], back[1], held)


def solution(mesh):
    in_specs = (
        P(None, ALL, None),
        P(None, ALL, None),
        P(("seq", "role"), None),
        P(("seq", "role"), None),
        P(),
        P(),
        P(),
        P(ALL, None, None),
        P(ALL, None, None),
    )
    return jax.shard_map(
        body, mesh=mesh, in_specs=in_specs, out_specs=P(None, ALL, None), check_vma=False
    )
```

profile of v0, /device:TPU:1, one launch (start us, length us, event | category | flops | bytes accessed | tf_op | source)
XLA Modules:
  0.0 171.8 jit_solution(1556009526511290754)
XLA Ops:
  0.0 0.9 fusion
  1.0 2.5 %collective-permute-start = (bf16[48,1536]{1,0:T(8,128)(2,1)S(1)}, bf16[48,1536]{1,0:T(8,128)(2,1)S(1)}, u32[]{:S(2)}, u32[]{:S(2)}) collective-permute-start(bf16[48,1536]{1,0:T(8,128)(2,1)S(1)} %maximum_select_fusion), channel_id=1, source_target_pairs={{0,32},{1,9},{2,34},{3,11},{4,36},{5,13},{6,38},{7,15},{8,40},{9,1... | collective-permute-start | bytes 442376 | tf_op jit(solution)/shard_map/ppermute | solution.py:316
  3.5 2.2 %collective-permute-start.1 = (bf16[48,1536]{1,0:T(8,128)(2,1)S(1)}, bf16[48,1536]{1,0:T(8,128)(2,1)S(1)}, u32[]{:S(2)}, u32[]{:S(2)}) collective-permute-start(bf16[48,1536]{1,0:T(8,128)(2,1)S(1)} %maximum_select_fusion), channel_id=1, source_target_pairs={{0,96},{1,25},{2,98},{3,27},{4,100},{5,29},{6,102},{7,31},{8,104},... | collective-permute-start | bytes 442376 | tf_op jit(solution)/shard_map/ppermute | solution.py:316
  5.7 1.2 collective-permute-start.2
  6.9 1.5 collective-permute-done
  8.4 3.1 %collective-permute-done.2 = bf16[48,1536]{1,0:T(8,128)(2,1)S(1)} collective-permute-done((bf16[48,1536]{1,0:T(8,128)(2,1)S(1)}, bf16[48,1536]{1,0:T(8,128)(2,1)S(1)}, u32[]{:S(2)}, u32[]{:S(2)}) %collective-permute-start.2) | collective-permute-done | bytes 147488 | tf_op jit(solution)/shard_map/ppermute | solution.py:316
  11.6 1.0 collective-permute-start.3
  12.6 1.8 %collective-permute-start.4 = (bf16[192,1536]{1,0:T(8,128)(2,1)S(1)}, bf16[192,1536]{1,0:T(8,128)(2,1)S(1)}, u32[]{:S(2)}, u32[]{:S(2)}) collective-permute-start(bf16[192,1536]{1,0:T(8,128)(2,1)S(1)} %pad_maximum_fusion.m0.b0), channel_id=1, source_target_pairs={{0,24},{1,97},{2,26},{3,99},{4,28},{5,101},{6,30},{7,103},{8,0},{9... | collective-permute-start | bytes 1769480 | tf_op jit(solution)/shard_map/ppermute | solution.py:317
  14.3 1.2 collective-permute-start.5
  15.6 6.3 %collective-permute-done.3 = bf16[192,1536]{1,0:T(8,128)(2,1)S(1)} collective-permute-done((bf16[192,1536]{1,0:T(8,128)(2,1)S(1)}, bf16[192,1536]{1,0:T(8,128)(2,1)S(1)}, u32[]{:S(2)}, u32[]{:S(2)}) %collective-permute-start.3) | collective-permute-done | bytes 589856 | tf_op jit(solution)/shard_map/ppermute | solution.py:317
  21.9 5.5 %collective-permute-done.4 = bf16[192,1536]{1,0:T(8,128)(2,1)S(1)} collective-permute-done((bf16[192,1536]{1,0:T(8,128)(2,1)S(1)}, bf16[192,1536]{1,0:T(8,128)(2,1)S(1)}, u32[]{:S(2)}, u32[]{:S(2)}) %collective-permute-start.4) | collective-permute-done | bytes 589856 | tf_op jit(solution)/shard_map/ppermute | solution.py:317
  27.5 1.4 collective-permute-done.5
  28.9 3.4 %collective-permute-start.7 = (bf16[576,1536]{1,0:T(8,128)(2,1)S(1)}, bf16[576,1536]{1,0:T(8,128)(2,1)S(1)}, u32[]{:S(2)}, u32[]{:S(2)}) collective-permute-start(bf16[576,1536]{1,0:T(8,128)(2,1)S(1)} %constant_dynamic-update-slice_fusion.m1.b1), channel_id=1, source_target_pairs={{0,1},{1,0},{2,3},{3,2},{4,5},{5,4},{6,7},{7,6},{8,9},{9,8},{10,11... | collective-permute-start | bytes 5308424 | tf_op jit(solution)/shard_map/ppermute | solution.py:319
  32.7 4.5 %first_half.1 = (bf16[512,384]{1,0:T(8,128)(2,1)S(1)}, bf16[512,768]{1,0:T(8,128)(2,1)S(1)}) custom-call(bf16[2,512,768]{2,1,0:T(8,128)(2,1)S(1)} %copy-done, f32[768]{0:T(1024)S(1)} %copy-done.8, bf16[192,1536]{1,0:T(8,128)(2,1)S(1)} %pad_maximum_fusion.m0.b0, bf16[576,1536]{1,0:T(8,128)(2,1)S(1)} %constant_dynamic-update-slice_fusion.m1.b1), custom_call_target="tpu_custom_call" | custom-call | tf_op jit(solution)/shard_map/first_half/pallas_call | solution.py:338
  37.2 1.2 copy-done.3
  38.4 1.5 copy-done.4
  39.9 8.0 %second_half.1 = (bf16[512,768]{1,0:T(8,128)(2,1)}, bf16[128,8,768]{2,1,0:T(8,128)(2,1)}, f32[512,128]{1,0:T(8,128)}) custom-call(bf16[2,512,768]{2,1,0:T(8,128)(2,1)} %x_ref.5, bf16[512,768]{1,0:T(8,128)(2,1)S(1)} %get-tuple-element.16.normed_ref, bf16[192,1536]{1,0:T(8,128)(2,1)S(1)} %pad_maximum_fusion.m0.b0, ...), custom_call_target="tpu_custom_call" | custom-call | tf_op jit(solution)/shard_map/second_half/pallas_call | solution.py:381
  47.9 0.8 copy-done.6
  48.7 7.3 %all-to-all-start.2 = ((bf16[128,8,768]{2,1,0:T(8,128)(2,1)}), bf16[128,8,768]{2,1,0:T(8,128)(2,1)}, u32[]{:S(2)}, u32[]{:S(2)}) async-start(bf16[128,8,768]{2,1,0:T(8,128)(2,1)} %get-tuple-element.20), calls=%async_computation.2 | async-start | bytes 3145728 | tf_op jit(solution)/shard_map/all_to_all | solution.py:402
  56.1 1.5 copy-done.5
  57.5 12.4 %whole.1 = (bf16[512,768]{1,0:T(8,128)(2,1)}, bf16[128,8,768]{2,1,0:T(8,128)(2,1)}, f32[512,128]{1,0:T(8,128)}) custom-call(bf16[2,512,768]{2,1,0:T(8,128)(2,1)} %x_ref.5, f32[768]{0:T(1024)} %gain_ref.4, bf16[192,1536]{1,0:T(8,128)(2,1)S(1)} %copy-done.2, bf16[576,1536]{1,0:T(8,128)(2,1)S(1)} %constant_dynamic-update-slice_fusion.m1.b1, ...), custom_call_target="tpu_custom_call" | custom-call | tf_op jit(solution)/shard_map/whole/pallas_call | solution.py:391
  70.0 10.3 %all-to-all-done.2.x_ref = bf16[128,8,768]{2,1,0:T(8,128)(2,1)} async-done(((bf16[128,8,768]{2,1,0:T(8,128)(2,1)}), bf16[128,8,768]{2,1,0:T(8,128)(2,1)}, u32[]{:S(2)}, u32[]{:S(2)}) %all-to-all-start.2) | async-done | bytes 1572896 | tf_op jit(solution)/shard_map/all_to_all | solution.py:402
  80.3 4.7 %all-to-all-start = ((bf16[128,8,768]{2,1,0:T(8,128)(2,1)}), bf16[128,8,768]{2,1,0:T(8,128)(2,1)S(1)}, u32[]{:S(2)}, u32[]{:S(2)}) async-start(bf16[128,8,768]{2,1,0:T(8,128)(2,1)} %get-tuple-element.15), calls=%async_computation | async-start | bytes 3145728 | tf_op jit(solution)/shard_map/all_to_all | solution.py:402
  85.0 14.3 %expert.3 = bf16[128,8,768]{2,1,0:T(8,128)(2,1)} custom-call(bf16[128,8,768]{2,1,0:T(8,128)(2,1)} %all-to-all-done.2.x_ref, bf16[1,768,3072]{2,1,0:T(8,128)(2,1)} %in_ref.3, bf16[1,3072,768]{2,1,0:T(8,128)(2,1)} %out_ref.3), custom_call_target="tpu_custom_call" | custom-call | tf_op jit(solution)/shard_map/expert/pallas_call | solution.py:408
  99.3 10.4 %all-to-all-done.x_ref = bf16[128,8,768]{2,1,0:T(8,128)(2,1)S(1)} async-done(((bf16[128,8,768]{2,1,0:T(8,128)(2,1)}), bf16[128,8,768]{2,1,0:T(8,128)(2,1)S(1)}, u32[]{:S(2)}, u32[]{:S(2)}) %all-to-all-start) | async-done | bytes 1572896 | tf_op jit(solution)/shard_map/all_to_all | solution.py:402
  109.7 4.7 %all-to-all-start.3 = ((bf16[128,8,768]{2,1,0:T(8,128)(2,1)}), bf16[128,8,768]{2,1,0:T(8,128)(2,1)S(1)}, u32[]{:S(2)}, u32[]{:S(2)}) async-start(bf16[128,8,768]{2,1,0:T(8,128)(2,1)} %expert.3), calls=%async_computation.3 | async-start | bytes 3145728 | tf_op jit(solution)/shard_map/all_to_all | solution.py:402
  114.4 13.8 %expert.2 = bf16[128,8,768]{2,1,0:T(8,128)(2,1)} custom-call(bf16[128,8,768]{2,1,0:T(8,128)(2,1)S(1)} %all-to-all-done.x_ref, bf16[1,768,3072]{2,1,0:T(8,128)(2,1)} %in_ref.3, bf16[1,3072,768]{2,1,0:T(8,128)(2,1)} %out_ref.3), custom_call_target="tpu_custom_call" | custom-call | tf_op jit(solution)/shard_map/expert/pallas_call | solution.py:408
  128.2 10.9 %all-to-all-done.3.back_ref = bf16[128,8,768]{2,1,0:T(8,128)(2,1)S(1)} async-done(((bf16[128,8,768]{2,1,0:T(8,128)(2,1)}), bf16[128,8,768]{2,1,0:T(8,128)(2,1)S(1)}, u32[]{:S(2)}, u32[]{:S(2)}) %all-to-all-start.3) | async-done | bytes 1572896 | tf_op jit(solution)/shard_map/all_to_all | solution.py:402
  139.1 4.7 %all-to-all-start.1 = ((bf16[128,8,768]{2,1,0:T(8,128)(2,1)}), bf16[128,8,768]{2,1,0:T(8,128)(2,1)S(1)}, u32[]{:S(2)}, u32[]{:S(2)}) async-start(bf16[128,8,768]{2,1,0:T(8,128)(2,1)} %expert.2), calls=%async_computation.1 | async-start | bytes 3145728 | tf_op jit(solution)/shard_map/all_to_all | solution.py:402
  143.8 3.1 %combine0.1.held_ref = bf16[2,512,768]{2,1,0:T(8,128)(2,1)} custom-call(bf16[512,768]{1,0:T(8,128)(2,1)} %get-tuple-element.18.att_ref, f32[512,128]{1,0:T(8,128)} %get-tuple-element.19.aux_ref, bf16[128,8,768]{2,1,0:T(8,128)(2,1)S(1)} %all-to-all-done.3.back_ref), custom_call_target="tpu_custom_call" | custom-call | tf_op jit(solution)/shard_map/combine0/pallas_call | solution.py:433
  146.9 21.6 %all-to-all-done.1.back_ref = bf16[128,8,768]{2,1,0:T(8,128)(2,1)S(1)} async-done(((bf16[128,8,768]{2,1,0:T(8,128)(2,1)}), bf16[128,8,768]{2,1,0:T(8,128)(2,1)S(1)}, u32[]{:S(2)}, u32[]{:S(2)}) %all-to-all-start.1) | async-done | bytes 1572896 | tf_op jit(solution)/shard_map/all_to_all | solution.py:402
  168.5 3.1 %combine1.1 = bf16[2,512,768]{2,1,0:T(8,128)(2,1)} custom-call(bf16[512,768]{1,0:T(8,128)(2,1)} %get-tuple-element.13.att_ref, f32[512,128]{1,0:T(8,128)} %get-tuple-element.14.aux_ref, bf16[128,8,768]{2,1,0:T(8,128)(2,1)S(1)} %all-to-all-done.1.back_ref, bf16[2,512,768]{2,1,0:T(8,128)(2,1)} %combine0.1.held_ref), custom_call_target="tpu_custom_call", output_to_operand_aliasing={{}: (3, {})} | custom-call | tf_op jit(solution)/shard_map/combine1/pallas_call | solution.py:442
  (23 shorter events, 0.5 us)
Async XLA Ops:
  1.0 7.4 %collective-permute-start = (bf16[48,1536]{1,0:T(8,128)(2,1)S(1)}, bf16[48,1536]{1,0:T(8,128)(2,1)S(1)}, u32[]{:S(2)}, u32[]{:S(2)}) collective-permute-start(bf16[48,1536]{1,0:T(8,128)(2,1)S(1)} %maximum_select_fusion), channel_id=1, source_target_pairs={{0,32},{1,9},{2,34},{3,11},{4,36},{5,13},{6,38},{7,15},{8,40},{9,1... | collective-permute-start | bytes 442376 | tf_op jit(solution)/shard_map/ppermute | solution.py:316
  3.5 4.9 %collective-permute-start.1 = (bf16[48,1536]{1,0:T(8,128)(2,1)S(1)}, bf16[48,1536]{1,0:T(8,128)(2,1)S(1)}, u32[]{:S(2)}, u32[]{:S(2)}) collective-permute-start(bf16[48,1536]{1,0:T(8,128)(2,1)S(1)} %maximum_select_fusion), channel_id=1, source_target_pairs={{0,96},{1,25},{2,98},{3,27},{4,100},{5,29},{6,102},{7,31},{8,104},... | collective-permute-start | bytes 442376 | tf_op jit(solution)/shard_map/ppermute | solution.py:316
  5.7 5.8 %collective-permute-start.2 = (bf16[48,1536]{1,0:T(8,128)(2,1)S(1)}, bf16[48,1536]{1,0:T(8,128)(2,1)S(1)}, u32[]{:S(2)}, u32[]{:S(2)}) collective-permute-start(bf16[48,1536]{1,0:T(8,128)(2,1)S(1)} %maximum_select_fusion), channel_id=1, source_target_pairs={{0,64},{1,17},{2,66},{3,19},{4,68},{5,21},{6,70},{7,23},{8,72},{9,... | collective-permute-start | bytes 442376 | tf_op jit(solution)/shard_map/ppermute | solution.py:316
  11.5 26.9 %copy-start.1 = (bf16[192,1536]{1,0:T(8,128)(2,1)}, bf16[192,1536]{1,0:T(8,128)(2,1)S(1)}, u32[]{:S(2)}) copy-start(bf16[192,1536]{1,0:T(8,128)(2,1)S(1)} %pad_maximum_fusion.m0.b0) | copy-start | bytes 1769476
  11.6 21.1 %copy-start = (bf16[2,512,768]{2,1,0:T(8,128)(2,1)S(1)}, bf16[2,512,768]{2,1,0:T(8,128)(2,1)}, u32[]{:S(2)}) copy-start(bf16[2,512,768]{2,1,0:T(8,128)(2,1)} %x_ref.5) | copy-start | bytes 4718596
  11.6 21.1 %copy-start.8 = (f32[768]{0:T(1024)S(1)}, f32[768]{0:T(1024)}, u32[]{:S(2)}) copy-start(f32[768]{0:T(1024)} %gain_ref.4) | copy-start | bytes 9220
  11.6 10.3 %collective-permute-start.3 = (bf16[192,1536]{1,0:T(8,128)(2,1)S(1)}, bf16[192,1536]{1,0:T(8,128)(2,1)S(1)}, u32[]{:S(2)}, u32[]{:S(2)}) collective-permute-start(bf16[192,1536]{1,0:T(8,128)(2,1)S(1)} %pad_maximum_fusion.m0.b0), channel_id=1, source_target_pairs={{0,8},{1,33},{2,10},{3,35},{4,12},{5,37},{6,14},{7,39},{8,16},{9,4... | collective-permute-start | bytes 1769480 | tf_op jit(solution)/shard_map/ppermute | solution.py:317
  12.6 14.9 %collective-permute-start.4 = (bf16[192,1536]{1,0:T(8,128)(2,1)S(1)}, bf16[192,1536]{1,0:T(8,128)(2,1)S(1)}, u32[]{:S(2)}, u32[]{:S(2)}) collective-permute-start(bf16[192,1536]{1,0:T(8,128)(2,1)S(1)} %pad_maximum_fusion.m0.b0), channel_id=1, source_target_pairs={{0,24},{1,97},{2,26},{3,99},{4,28},{5,101},{6,30},{7,103},{8,0},{9... | collective-permute-start | bytes 1769480 | tf_op jit(solution)/shard_map/ppermute | solution.py:317
  14.3 14.6 %collective-permute-start.5 = (bf16[192,1536]{1,0:T(8,128)(2,1)S(1)}, bf16[192,1536]{1,0:T(8,128)(2,1)S(1)}, u32[]{:S(2)}, u32[]{:S(2)}) collective-permute-start(bf16[192,1536]{1,0:T(8,128)(2,1)S(1)} %pad_maximum_fusion.m0.b0), channel_id=1, source_target_pairs={{0,16},{1,65},{2,18},{3,67},{4,20},{5,69},{6,22},{7,71},{8,24},{9,... | collective-permute-start | bytes 1769480 | tf_op jit(solution)/shard_map/ppermute | solution.py:317
  28.9 8.2 %collective-permute-start.7 = (bf16[576,1536]{1,0:T(8,128)(2,1)S(1)}, bf16[576,1536]{1,0:T(8,128)(2,1)S(1)}, u32[]{:S(2)}, u32[]{:S(2)}) collective-permute-start(bf16[576,1536]{1,0:T(8,128)(2,1)S(1)} %constant_dynamic-update-slice_fusion.m1.b1), channel_id=1, source_target_pairs={{0,1},{1,0},{2,3},{3,2},{4,5},{5,4},{6,7},{7,6},{8,9},{9,8},{10,11... | collective-permute-start | bytes 5308424 | tf_op jit(solution)/shard_map/ppermute | solution.py:319
  32.4 4.8 %collective-permute-start.6 = (bf16[192,1536]{1,0:T(8,128)(2,1)S(1)}, bf16[192,1536]{1,0:T(8,128)(2,1)S(1)}, u32[]{:S(2)}, u32[]{:S(2)}) collective-permute-start(bf16[192,1536]{1,0:T(8,128)(2,1)S(1)} %pad_maximum_fusion.m0.b0), channel_id=1, source_target_pairs={{0,1},{1,0},{2,3},{3,2},{4,5},{5,4},{6,7},{7,6},{8,9},{9,8},{10,11... | collective-permute-start | bytes 1769480 | tf_op jit(solution)/shard_map/ppermute | solution.py:319
  37.2 1.2 copy-start.3
  38.4 1.5 copy-start.4
  47.9 0.8 copy-start.6
  48.7 7.3 %copy-start.2 = (bf16[192,1536]{1,0:T(8,128)(2,1)S(1)}, bf16[192,1536]{1,0:T(8,128)(2,1)}, u32[]{:S(2)}) copy-start(bf16[192,1536]{1,0:T(8,128)(2,1)} %copy-done.1) | copy-start | bytes 1769476
  48.7 7.3 %copy-start.7 = (bf16[192,1536]{1,0:T(8,128)(2,1)S(1)}, bf16[192,1536]{1,0:T(8,128)(2,1)}, u32[]{:S(2)}) copy-start(bf16[192,1536]{1,0:T(8,128)(2,1)} %copy-done.6) | copy-start | bytes 1769476
  48.7 31.6 %all-to-all-start.2 = ((bf16[128,8,768]{2,1,0:T(8,128)(2,1)}), bf16[128,8,768]{2,1,0:T(8,128)(2,1)}, u32[]{:S(2)}, u32[]{:S(2)}) async-start(bf16[128,8,768]{2,1,0:T(8,128)(2,1)} %get-tuple-element.20), calls=%async_computation.2 | async-start | bytes 3145728 | tf_op jit(solution)/shard_map/all_to_all | solution.py:402
  56.0 1.5 copy-start.5
  80.3 29.4 %all-to-all-start = ((bf16[128,8,768]{2,1,0:T(8,128)(2,1)}), bf16[128,8,768]{2,1,0:T(8,128)(2,1)S(1)}, u32[]{:S(2)}, u32[]{:S(2)}) async-start(bf16[128,8,768]{2,1,0:T(8,128)(2,1)} %get-tuple-element.15), calls=%async_computation | async-start | bytes 3145728 | tf_op jit(solution)/shard_map/all_to_all | solution.py:402
  109.7 29.4 %all-to-all-start.3 = ((bf16[128,8,768]{2,1,0:T(8,128)(2,1)}), bf16[128,8,768]{2,1,0:T(8,128)(2,1)S(1)}, u32[]{:S(2)}, u32[]{:S(2)}) async-start(bf16[128,8,768]{2,1,0:T(8,128)(2,1)} %expert.3), calls=%async_computation.3 | async-start | bytes 3145728 | tf_op jit(solution)/shard_map/all_to_all | solution.py:402
  139.1 29.4 %all-to-all-start.1 = ((bf16[128,8,768]{2,1,0:T(8,128)(2,1)}), bf16[128,8,768]{2,1,0:T(8,128)(2,1)S(1)}, u32[]{:S(2)}, u32[]{:S(2)}) async-start(bf16[128,8,768]{2,1,0:T(8,128)(2,1)} %expert.2), calls=%async_computation.1 | async-start | bytes 3145728 | tf_op jit(solution)/shard_map/all_to_all | solution.py:402
where the time goes:
time: 172 us
  waiting for transfers between devices  71 us (41%)
  Pallas kernels  59.3 us (34%)
  starting transfers between devices  35 us (20%)
  local copies, waits for them, and re-layouts  6.08 us (4%)
    all_to_all x4, waiting for transfers between devices, exchange(): moved = lax.all_to_all(values, ALL, split_axis=0, concat_axis=0, tiled=True)  53.2 us
    pallas_call x2, Pallas kernels, serve(): pl.pallas_call(expert_kernel, grid=(hidden // chunk,), out_shape=jax.Shap...  28.2 us
    all_to_all x4, starting transfers between devices, exchange(): moved = lax.all_to_all(values, ALL, split_axis=0, concat_axis=0, tiled=True)  21.4 us
    ppermute x3, waiting for transfers between devices, body(): lax.ppermute(own, ALL, hop(d, 1))  13.2 us
    pallas_call x1, Pallas kernels, body(): pl.pallas_call(whole_kernel, out_shape=finish_out, in_specs=[any_spec] *...  12.4 us
    pallas_call x1, Pallas kernels, body(): pl.pallas_call(second_half_kernel, out_shape=finish_out, in_specs=[any_sp...  7.97 us
    ppermute x3, starting transfers between devices, body(): lax.ppermute(piece, ALL, hop(d, 0))  5.95 us
    unnamed x20, local copies, waits for them, and re-layouts  5.12 us
  transfers between devices with their start and end apart: 12, of which 9 were waited for; matrix products, arithmetic and copies ran while one was open for 0% of the time, Pallas kernels for 28%

commit v1 on v0

--- a/solution.py
+++ b/solution.py
@@ -384,7 +384,7 @@
         in_specs=[any_spec] + [whole] * 6 + [any_spec] * 3,
         out_specs=finish_specs,
         scratch_shapes=scratch,
-        compiler_params=limit(55900),
+        compiler_params=limit(54000),
         name="second_half",
     )(tokens, near(normed), *mine, *other, near(ctx_mine), norm_ffn, router, ids_row)
 
@@ -394,7 +394,7 @@
         in_specs=[any_spec] * 2 + [whole] * 4 + [any_spec] * 3,
         out_specs=finish_specs,
         scratch_shapes=[gain_scratch] + scratch,
-        compiler_params=limit(55500),
+        compiler_params=limit(54000),
         name="whole",
     )(tokens, norm_attn, *mine, *other, norm_ffn, router, ids_row)
 

time: 172 us -> 169 us (0.983)
  local copies, waits for them, and re-layouts: 6.08 us -> 2.55 us
    unnamed x20 -> x18, local copies, waits for them, and re-layouts: 5.12 us -> 1.59 us
  transfers between devices with their start and end apart: 12 -> 12, of which waited for: 9 -> 9; matrix products, arithmetic and copies ran while one was open for 0% -> 0% of each run, Pallas kernels for 28% -> 29%
where the time goes in v1:
time: 169 us; the launch traced here: 168 us
  waiting for transfers between devices  71 us (42%)
  Pallas kernels  59.4 us (35%)
  starting transfers between devices  35 us (21%)
  local copies, waits for them, and re-layouts  2.55 us (2%)
    all_to_all x4, waiting for transfers between devices, exchange(): moved = lax.all_to_all(values, ALL, split_axis=0, concat_axis=0, tiled=True)  53.2 us
    pallas_call x2, Pallas kernels, serve(): pl.pallas_call(expert_kernel, grid=(hidden // chunk,), out_shape=jax.Shap...  28.2 us
    all_to_all x4, starting transfers between devices, exchange(): moved = lax.all_to_all(values, ALL, split_axis=0, concat_axis=0, tiled=True)  21.4 us
    ppermute x3, waiting for transfers between devices, body(): lax.ppermute(own, ALL, hop(d, 1))  13.2 us
    pallas_call x1, Pallas kernels, body(): pl.pallas_call(whole_kernel, out_shape=finish_out, in_specs=[any_spec] *...  12.4 us
    pallas_call x1, Pallas kernels, body(): pl.pallas_call(second_half_kernel, out_shape=finish_out, in_specs=[any_sp...  8.08 us
    ppermute x3, starting transfers between devices, body(): lax.ppermute(piece, ALL, hop(d, 0))  5.95 us
    ppermute x3, waiting for transfers between devices, body(): lax.ppermute(piece, ALL, hop(d, 0))  4.57 us
  transfers between devices with their start and end apart: 12, of which 9 were waited for; matrix products, arithmetic and copies ran while one was open for 0% of the time, Pallas kernels for 29%

profile of v1, /device:TPU:1, one launch (start us, length us, event | category | flops | bytes accessed | tf_op | source)
XLA Modules:
  0.0 168.4 jit_solution(14485037794872493994)
XLA Ops:
  0.0 0.9 fusion
  1.0 2.5 %collective-permute-start = (bf16[48,1536]{1,0:T(8,128)(2,1)S(1)}, bf16[48,1536]{1,0:T(8,128)(2,1)S(1)}, u32[]{:S(2)}, u32[]{:S(2)}) collective-permute-start(bf16[48,1536]{1,0:T(8,128)(2,1)S(1)} %maximum_select_fusion), channel_id=1, source_target_pairs={{0,32},{1,9},{2,34},{3,11},{4,36},{5,13},{6,38},{7,15},{8,40},{9,1... | collective-permute-start | bytes 442376 | tf_op jit(solution)/shard_map/ppermute | solution.py:316
  3.5 2.2 %collective-permute-start.1 = (bf16[48,1536]{1,0:T(8,128)(2,1)S(1)}, bf16[48,1536]{1,0:T(8,128)(2,1)S(1)}, u32[]{:S(2)}, u32[]{:S(2)}) collective-permute-start(bf16[48,1536]{1,0:T(8,128)(2,1)S(1)} %maximum_select_fusion), channel_id=1, source_target_pairs={{0,96},{1,25},{2,98},{3,27},{4,100},{5,29},{6,102},{7,31},{8,104},... | collective-permute-start | bytes 442376 | tf_op jit(solution)/shard_map/ppermute | solution.py:316
  5.7 1.2 collective-permute-start.2
  6.9 1.5 collective-permute-done
  8.4 3.1 %collective-permute-done.2 = bf16[48,1536]{1,0:T(8,128)(2,1)S(1)} collective-permute-done((bf16[48,1536]{1,0:T(8,128)(2,1)S(1)}, bf16[48,1536]{1,0:T(8,128)(2,1)S(1)}, u32[]{:S(2)}, u32[]{:S(2)}) %collective-permute-start.2) | collective-permute-done | bytes 147488 | tf_op jit(solution)/shard_map/ppermute | solution.py:316
  11.6 0.0 copy-start.7
  11.6 1.0 collective-permute-start.3
  12.6 1.8 %collective-permute-start.4 = (bf16[192,1536]{1,0:T(8,128)(2,1)S(1)}, bf16[192,1536]{1,0:T(8,128)(2,1)S(1)}, u32[]{:S(2)}, u32[]{:S(2)}) collective-permute-start(bf16[192,1536]{1,0:T(8,128)(2,1)S(1)} %pad_maximum_fusion.m0.b0), channel_id=1, source_target_pairs={{0,24},{1,97},{2,26},{3,99},{4,28},{5,101},{6,30},{7,103},{8,0},{9... | collective-permute-start | bytes 1769480 | tf_op jit(solution)/shard_map/ppermute | solution.py:317
  14.3 1.2 collective-permute-start.5
  15.6 6.3 %collective-permute-done.3 = bf16[192,1536]{1,0:T(8,128)(2,1)S(1)} collective-permute-done((bf16[192,1536]{1,0:T(8,128)(2,1)S(1)}, bf16[192,1536]{1,0:T(8,128)(2,1)S(1)}, u32[]{:S(2)}, u32[]{:S(2)}) %collective-permute-start.3) | collective-permute-done | bytes 589856 | tf_op jit(solution)/shard_map/ppermute | solution.py:317
  21.9 5.5 %collective-permute-done.4 = bf16[192,1536]{1,0:T(8,128)(2,1)S(1)} collective-permute-done((bf16[192,1536]{1,0:T(8,128)(2,1)S(1)}, bf16[192,1536]{1,0:T(8,128)(2,1)S(1)}, u32[]{:S(2)}, u32[]{:S(2)}) %collective-permute-start.4) | collective-permute-done | bytes 589856 | tf_op jit(solution)/shard_map/ppermute | solution.py:317
  27.5 1.4 collective-permute-done.5
  28.9 3.4 %collective-permute-start.7 = (bf16[576,1536]{1,0:T(8,128)(2,1)S(1)}, bf16[576,1536]{1,0:T(8,128)(2,1)S(1)}, u32[]{:S(2)}, u32[]{:S(2)}) collective-permute-start(bf16[576,1536]{1,0:T(8,128)(2,1)S(1)} %constant_dynamic-update-slice_fusion.m1.b1), channel_id=1, source_target_pairs={{0,1},{1,0},{2,3},{3,2},{4,5},{5,4},{6,7},{7,6},{8,9},{9,8},{10,11... | collective-permute-start | bytes 5308424 | tf_op jit(solution)/shard_map/ppermute | solution.py:319
  32.4 0.3 collective-permute-start.6
  32.7 4.5 %first_half.1 = (bf16[512,384]{1,0:T(8,128)(2,1)S(1)}, bf16[512,768]{1,0:T(8,128)(2,1)S(1)}) custom-call(bf16[2,512,768]{2,1,0:T(8,128)(2,1)S(1)} %copy-done, f32[768]{0:T(1024)S(1)} %copy-done.7, bf16[192,1536]{1,0:T(8,128)(2,1)S(1)} %pad_maximum_fusion.m0.b0, bf16[576,1536]{1,0:T(8,128)(2,1)S(1)} %constant_dynamic-update-slice_fusion.m1.b1), custom_call_target="tpu_custom_call" | custom-call | tf_op jit(solution)/shard_map/first_half/pallas_call | solution.py:338
  37.2 8.1 %second_half.1 = (bf16[512,768]{1,0:T(8,128)(2,1)}, bf16[128,8,768]{2,1,0:T(8,128)(2,1)}, f32[512,128]{1,0:T(8,128)}) custom-call(bf16[2,512,768]{2,1,0:T(8,128)(2,1)} %x_ref.5, bf16[512,768]{1,0:T(8,128)(2,1)S(1)} %get-tuple-element.16.normed_ref, bf16[192,1536]{1,0:T(8,128)(2,1)S(1)} %pad_maximum_fusion.m0.b0, ...), custom_call_target="tpu_custom_call" | custom-call | tf_op jit(solution)/shard_map/second_half/pallas_call | solution.py:381
  45.3 0.0 copy-start.2
  45.3 7.3 %all-to-all-start.2 = ((bf16[128,8,768]{2,1,0:T(8,128)(2,1)}), bf16[128,8,768]{2,1,0:T(8,128)(2,1)}, u32[]{:S(2)}, u32[]{:S(2)}) async-start(bf16[128,8,768]{2,1,0:T(8,128)(2,1)} %get-tuple-element.20), calls=%async_computation.2 | async-start | bytes 3145728 | tf_op jit(solution)/shard_map/all_to_all | solution.py:402
  52.7 1.5 copy-done.4
  54.1 12.4 %whole.1 = (bf16[512,768]{1,0:T(8,128)(2,1)}, bf16[128,8,768]{2,1,0:T(8,128)(2,1)}, f32[512,128]{1,0:T(8,128)}) custom-call(bf16[2,512,768]{2,1,0:T(8,128)(2,1)} %x_ref.5, f32[768]{0:T(1024)} %gain_ref.4, bf16[192,1536]{1,0:T(8,128)(2,1)S(1)} %copy-done.2, bf16[576,1536]{1,0:T(8,128)(2,1)S(1)} %constant_dynamic-update-slice_fusion.m1.b1, ...), custom_call_target="tpu_custom_call" | custom-call | tf_op jit(solution)/shard_map/whole/pallas_call | solution.py:391
  66.6 10.3 %all-to-all-done.2.x_ref = bf16[128,8,768]{2,1,0:T(8,128)(2,1)} async-done(((bf16[128,8,768]{2,1,0:T(8,128)(2,1)}), bf16[128,8,768]{2,1,0:T(8,128)(2,1)}, u32[]{:S(2)}, u32[]{:S(2)}) %all-to-all-start.2) | async-done | bytes 1572896 | tf_op jit(solution)/shard_map/all_to_all | solution.py:402
  76.9 4.7 %all-to-all-start = ((bf16[128,8,768]{2,1,0:T(8,128)(2,1)}), bf16[128,8,768]{2,1,0:T(8,128)(2,1)S(1)}, u32[]{:S(2)}, u32[]{:S(2)}) async-start(bf16[128,8,768]{2,1,0:T(8,128)(2,1)} %get-tuple-element.15), calls=%async_computation | async-start | bytes 3145728 | tf_op jit(solution)/shard_map/all_to_all | solution.py:402
  81.6 14.4 %expert.3 = bf16[128,8,768]{2,1,0:T(8,128)(2,1)} custom-call(bf16[128,8,768]{2,1,0:T(8,128)(2,1)} %all-to-all-done.2.x_ref, bf16[1,768,3072]{2,1,0:T(8,128)(2,1)} %in_ref.3, bf16[1,3072,768]{2,1,0:T(8,128)(2,1)} %out_ref.3), custom_call_target="tpu_custom_call" | custom-call | tf_op jit(solution)/shard_map/expert/pallas_call | solution.py:408
  96.0 10.4 %all-to-all-done.x_ref = bf16[128,8,768]{2,1,0:T(8,128)(2,1)S(1)} async-done(((bf16[128,8,768]{2,1,0:T(8,128)(2,1)}), bf16[128,8,768]{2,1,0:T(8,128)(2,1)S(1)}, u32[]{:S(2)}, u32[]{:S(2)}) %all-to-all-start) | async-done | bytes 1572896 | tf_op jit(solution)/shard_map/all_to_all | solution.py:402
  106.3 4.7 %all-to-all-start.3 = ((bf16[128,8,768]{2,1,0:T(8,128)(2,1)}), bf16[128,8,768]{2,1,0:T(8,128)(2,1)S(1)}, u32[]{:S(2)}, u32[]{:S(2)}) async-start(bf16[128,8,768]{2,1,0:T(8,128)(2,1)} %expert.3), calls=%async_computation.3 | async-start | bytes 3145728 | tf_op jit(solution)/shard_map/all_to_all | solution.py:402
  111.0 13.8 %expert.2 = bf16[128,8,768]{2,1,0:T(8,128)(2,1)} custom-call(bf16[128,8,768]{2,1,0:T(8,128)(2,1)S(1)} %all-to-all-done.x_ref, bf16[1,768,3072]{2,1,0:T(8,128)(2,1)} %in_ref.3, bf16[1,3072,768]{2,1,0:T(8,128)(2,1)} %out_ref.3), custom_call_target="tpu_custom_call" | custom-call | tf_op jit(solution)/shard_map/expert/pallas_call | solution.py:408
  124.9 10.9 %all-to-all-done.3.back_ref = bf16[128,8,768]{2,1,0:T(8,128)(2,1)S(1)} async-done(((bf16[128,8,768]{2,1,0:T(8,128)(2,1)}), bf16[128,8,768]{2,1,0:T(8,128)(2,1)S(1)}, u32[]{:S(2)}, u32[]{:S(2)}) %all-to-all-start.3) | async-done | bytes 1572896 | tf_op jit(solution)/shard_map/all_to_all | solution.py:402
  135.7 4.7 %all-to-all-start.1 = ((bf16[128,8,768]{2,1,0:T(8,128)(2,1)}), bf16[128,8,768]{2,1,0:T(8,128)(2,1)S(1)}, u32[]{:S(2)}, u32[]{:S(2)}) async-start(bf16[128,8,768]{2,1,0:T(8,128)(2,1)} %expert.2), calls=%async_computation.1 | async-start | bytes 3145728 | tf_op jit(solution)/shard_map/all_to_all | solution.py:402
  140.4 3.1 %combine0.1.held_ref = bf16[2,512,768]{2,1,0:T(8,128)(2,1)} custom-call(bf16[512,768]{1,0:T(8,128)(2,1)} %get-tuple-element.18.att_ref, f32[512,128]{1,0:T(8,128)} %get-tuple-element.19.aux_ref, bf16[128,8,768]{2,1,0:T(8,128)(2,1)S(1)} %all-to-all-done.3.back_ref), custom_call_target="tpu_custom_call" | custom-call | tf_op jit(solution)/shard_map/combine0/pallas_call | solution.py:433
  143.5 21.6 %all-to-all-done.1.back_ref = bf16[128,8,768]{2,1,0:T(8,128)(2,1)S(1)} async-done(((bf16[128,8,768]{2,1,0:T(8,128)(2,1)}), bf16[128,8,768]{2,1,0:T(8,128)(2,1)S(1)}, u32[]{:S(2)}, u32[]{:S(2)}) %all-to-all-start.1) | async-done | bytes 1572896 | tf_op jit(solution)/shard_map/all_to_all | solution.py:402
  165.1 3.1 %combine1.1 = bf16[2,512,768]{2,1,0:T(8,128)(2,1)} custom-call(bf16[512,768]{1,0:T(8,128)(2,1)} %get-tuple-element.13.att_ref, f32[512,128]{1,0:T(8,128)} %get-tuple-element.14.aux_ref, bf16[128,8,768]{2,1,0:T(8,128)(2,1)S(1)} %all-to-all-done.1.back_ref, bf16[2,512,768]{2,1,0:T(8,128)(2,1)} %combine0.1.held_ref), custom_call_target="tpu_custom_call", output_to_operand_aliasing={{}: (3, {})} | custom-call | tf_op jit(solution)/shard_map/combine1/pallas_call | solution.py:442
  (21 shorter events, 0.2 us)
Async XLA Ops:
  1.0 7.4 %collective-permute-start = (bf16[48,1536]{1,0:T(8,128)(2,1)S(1)}, bf16[48,1536]{1,0:T(8,128)(2,1)S(1)}, u32[]{:S(2)}, u32[]{:S(2)}) collective-permute-start(bf16[48,1536]{1,0:T(8,128)(2,1)S(1)} %maximum_select_fusion), channel_id=1, source_target_pairs={{0,32},{1,9},{2,34},{3,11},{4,36},{5,13},{6,38},{7,15},{8,40},{9,1... | collective-permute-start | bytes 442376 | tf_op jit(solution)/shard_map/ppermute | solution.py:316
  3.5 4.9 %collective-permute-start.1 = (bf16[48,1536]{1,0:T(8,128)(2,1)S(1)}, bf16[48,1536]{1,0:T(8,128)(2,1)S(1)}, u32[]{:S(2)}, u32[]{:S(2)}) collective-permute-start(bf16[48,1536]{1,0:T(8,128)(2,1)S(1)} %maximum_select_fusion), channel_id=1, source_target_pairs={{0,96},{1,25},{2,98},{3,27},{4,100},{5,29},{6,102},{7,31},{8,104},... | collective-permute-start | bytes 442376 | tf_op jit(solution)/shard_map/ppermute | solution.py:316
  5.7 5.8 %collective-permute-start.2 = (bf16[48,1536]{1,0:T(8,128)(2,1)S(1)}, bf16[48,1536]{1,0:T(8,128)(2,1)S(1)}, u32[]{:S(2)}, u32[]{:S(2)}) collective-permute-start(bf16[48,1536]{1,0:T(8,128)(2,1)S(1)} %maximum_select_fusion), channel_id=1, source_target_pairs={{0,64},{1,17},{2,66},{3,19},{4,68},{5,21},{6,70},{7,23},{8,72},{9,... | collective-permute-start | bytes 442376 | tf_op jit(solution)/shard_map/ppermute | solution.py:316
  11.5 25.6 %copy-start.1 = (bf16[192,1536]{1,0:T(8,128)(2,1)}, bf16[192,1536]{1,0:T(8,128)(2,1)S(1)}, u32[]{:S(2)}) copy-start(bf16[192,1536]{1,0:T(8,128)(2,1)S(1)} %pad_maximum_fusion.m0.b0) | copy-start | bytes 1769476
  11.6 21.1 %copy-start = (bf16[2,512,768]{2,1,0:T(8,128)(2,1)S(1)}, bf16[2,512,768]{2,1,0:T(8,128)(2,1)}, u32[]{:S(2)}) copy-start(bf16[2,512,768]{2,1,0:T(8,128)(2,1)} %x_ref.5) | copy-start | bytes 4718596
  11.6 21.1 %copy-start.7 = (f32[768]{0:T(1024)S(1)}, f32[768]{0:T(1024)}, u32[]{:S(2)}) copy-start(f32[768]{0:T(1024)} %gain_ref.4) | copy-start | bytes 9220
  11.6 10.3 %collective-permute-start.3 = (bf16[192,1536]{1,0:T(8,128)(2,1)S(1)}, bf16[192,1536]{1,0:T(8,128)(2,1)S(1)}, u32[]{:S(2)}, u32[]{:S(2)}) collective-permute-start(bf16[192,1536]{1,0:T(8,128)(2,1)S(1)} %pad_maximum_fusion.m0.b0), channel_id=1, source_target_pairs={{0,8},{1,33},{2,10},{3,35},{4,12},{5,37},{6,14},{7,39},{8,16},{9,4... | collective-permute-start | bytes 1769480 | tf_op jit(solution)/shard_map/ppermute | solution.py:317
  12.6 14.9 %collective-permute-start.4 = (bf16[192,1536]{1,0:T(8,128)(2,1)S(1)}, bf16[192,1536]{1,0:T(8,128)(2,1)S(1)}, u32[]{:S(2)}, u32[]{:S(2)}) collective-permute-start(bf16[192,1536]{1,0:T(8,128)(2,1)S(1)} %pad_maximum_fusion.m0.b0), channel_id=1, source_target_pairs={{0,24},{1,97},{2,26},{3,99},{4,28},{5,101},{6,30},{7,103},{8,0},{9... | collective-permute-start | bytes 1769480 | tf_op jit(solution)/shard_map/ppermute | solution.py:317
  14.3 14.6 %collective-permute-start.5 = (bf16[192,1536]{1,0:T(8,128)(2,1)S(1)}, bf16[192,1536]{1,0:T(8,128)(2,1)S(1)}, u32[]{:S(2)}, u32[]{:S(2)}) collective-permute-start(bf16[192,1536]{1,0:T(8,128)(2,1)S(1)} %pad_maximum_fusion.m0.b0), channel_id=1, source_target_pairs={{0,16},{1,65},{2,18},{3,67},{4,20},{5,69},{6,22},{7,71},{8,24},{9,... | collective-permute-start | bytes 1769480 | tf_op jit(solution)/shard_map/ppermute | solution.py:317
  28.9 8.2 %collective-permute-start.7 = (bf16[576,1536]{1,0:T(8,128)(2,1)S(1)}, bf16[576,1536]{1,0:T(8,128)(2,1)S(1)}, u32[]{:S(2)}, u32[]{:S(2)}) collective-permute-start(bf16[576,1536]{1,0:T(8,128)(2,1)S(1)} %constant_dynamic-update-slice_fusion.m1.b1), channel_id=1, source_target_pairs={{0,1},{1,0},{2,3},{3,2},{4,5},{5,4},{6,7},{7,6},{8,9},{9,8},{10,11... | collective-permute-start | bytes 5308424 | tf_op jit(solution)/shard_map/ppermute | solution.py:319
  32.4 4.8 %collective-permute-start.6 = (bf16[192,1536]{1,0:T(8,128)(2,1)S(1)}, bf16[192,1536]{1,0:T(8,128)(2,1)S(1)}, u32[]{:S(2)}, u32[]{:S(2)}) collective-permute-start(bf16[192,1536]{1,0:T(8,128)(2,1)S(1)} %pad_maximum_fusion.m0.b0), channel_id=1, source_target_pairs={{0,1},{1,0},{2,3},{3,2},{4,5},{5,4},{6,7},{7,6},{8,9},{9,8},{10,11... | collective-permute-start | bytes 1769480 | tf_op jit(solution)/shard_map/ppermute | solution.py:319
  37.1 8.1 %copy-start.5 = (bf16[192,1536]{1,0:T(8,128)(2,1)}, bf16[192,1536]{1,0:T(8,128)(2,1)S(1)}, u32[]{:S(2)}) copy-start(bf16[192,1536]{1,0:T(8,128)(2,1)S(1)} %collective-permute-done.6.o0) | copy-start | bytes 1769476
  37.2 8.1 %copy-start.3 = (bf16[576,1536]{1,0:T(8,128)(2,1)}, bf16[576,1536]{1,0:T(8,128)(2,1)S(1)}, u32[]{:S(2)}) copy-start(bf16[576,1536]{1,0:T(8,128)(2,1)S(1)} %collective-permute-done.7.o1) | copy-start | bytes 5308420
  45.3 7.3 %copy-start.2 = (bf16[192,1536]{1,0:T(8,128)(2,1)S(1)}, bf16[192,1536]{1,0:T(8,128)(2,1)}, u32[]{:S(2)}) copy-start(bf16[192,1536]{1,0:T(8,128)(2,1)} %copy-done.1) | copy-start | bytes 1769476
  45.3 7.3 %copy-start.6 = (bf16[192,1536]{1,0:T(8,128)(2,1)S(1)}, bf16[192,1536]{1,0:T(8,128)(2,1)}, u32[]{:S(2)}) copy-start(bf16[192,1536]{1,0:T(8,128)(2,1)} %copy-done.5) | copy-start | bytes 1769476
  45.3 31.6 %all-to-all-start.2 = ((bf16[128,8,768]{2,1,0:T(8,128)(2,1)}), bf16[128,8,768]{2,1,0:T(8,128)(2,1)}, u32[]{:S(2)}, u32[]{:S(2)}) async-start(bf16[128,8,768]{2,1,0:T(8,128)(2,1)} %get-tuple-element.20), calls=%async_computation.2 | async-start | bytes 3145728 | tf_op jit(solution)/shard_map/all_to_all | solution.py:402
  52.7 1.5 copy-start.4
  76.9 29.4 %all-to-all-start = ((bf16[128,8,768]{2,1,0:T(8,128)(2,1)}), bf16[128,8,768]{2,1,0:T(8,128)(2,1)S(1)}, u32[]{:S(2)}, u32[]{:S(2)}) async-start(bf16[128,8,768]{2,1,0:T(8,128)(2,1)} %get-tuple-element.15), calls=%async_computation | async-start | bytes 3145728 | tf_op jit(solution)/shard_map/all_to_all | solution.py:402
  106.3 29.4 %all-to-all-start.3 = ((bf16[128,8,768]{2,1,0:T(8,128)(2,1)}), bf16[128,8,768]{2,1,0:T(8,128)(2,1)S(1)}, u32[]{:S(2)}, u32[]{:S(2)}) async-start(bf16[128,8,768]{2,1,0:T(8,128)(2,1)} %expert.3), calls=%async_computation.3 | async-start | bytes 3145728 | tf_op jit(solution)/shard_map/all_to_all | solution.py:402
  135.7 29.4 %all-to-all-start.1 = ((bf16[128,8,768]{2,1,0:T(8,128)(2,1)}), bf16[128,8,768]{2,1,0:T(8,128)(2,1)S(1)}, u32[]{:S(2)}, u32[]{:S(2)}) async-start(bf16[128,8,768]{2,1,0:T(8,128)(2,1)} %expert.2), calls=%async_computation.1 | async-start | bytes 3145728 | tf_op jit(solution)/shard_map/all_to_all | solution.py:402

commit v2 on v1

--- a/solution.py
+++ b/solution.py
@@ -9,6 +9,7 @@
 
 HEADS = 12
 HALF = 384
+EXPERTS = 128
 SLOTS = 8
 ALL = ("seq", "role", "exp")
 F32 = jnp.float32
@@ -119,16 +120,28 @@
             store(pair, row, jnp.where(low, outs[0], outs[1]).astype(BF16))
 
 
-def context_kernel(
-    x_ref, gain_ref, b0, b1, ctx_ref, normed_ref, x, gain, w, projected, sem, small
-):
+def prepare_kernel(x_ref, gain_ref, row_ref, normed_ref, position_ref):
+    rows = x_ref.shape[1]
+    normed_ref[0] = scale_rows(x_ref[0], gain_ref[...]).astype(BF16)
+    ids_row = row_ref[0]
+    i0 = lax.broadcasted_iota(jnp.int32, (rows, rows), 0)
+    i1 = lax.broadcasted_iota(jnp.int32, (rows, rows), 1)
+    picked = ids_row == lax.broadcasted_iota(jnp.int32, (EXPERTS, rows), 0)
+    running = jnp.dot(
+        picked.astype(F32).astype(BF16),
+        (i0 <= i1).astype(F32).astype(BF16),
+        preferred_element_type=F32,
+    )
+    rank = jnp.sum(jnp.where(picked, running, 0.0), 0, keepdims=True)
+    position_ref[0] = ids_row * SLOTS + rank.astype(jnp.int32) - 1
+
+
+def context_kernel(n_ref, b0, b1, ctx_ref, normed, w, projected, sem, small):
     core = my_core()
-    loads = start_all([(x_ref.at[0], x), (gain_ref, gain)], small)
+    loads = start_all([(n_ref.at[0], normed)], small)
     copies, _ = fetch((b0, b1), core, w, sem)
-    wait_all(loads)
-    normed_ref[...] = scale_rows(x[...], gain[...]).astype(BF16)
-    wait_all(copies)
-    project(normed_ref, w.at[core], projected)
+    wait_all(loads + copies)
+    project(normed, w.at[core], projected)
 
     def store(pair, row, context):
         ctx_ref[row : row + context.shape[0], pair * 128 : pair * 128 + 128] = context
@@ -137,7 +150,7 @@
 
 
 def finish(
-    x, ctx, wo, gain, router, ids, att_ref, out_ref, aux_ref, normed, sent, att, aux, sems
+    x, ctx, wo, gain, router, ids, place_row, att_ref, out_ref, aux_ref, normed, sent, att, aux, sems
 ):
     rows, experts = x.shape[0], router.shape[1]
     block = 256
@@ -154,17 +167,9 @@
     logits = lax.dot_general(
         router[...], normed[...], (((0,), (1,)), ((), ())), preferred_element_type=F32
     )
-    i0 = lax.broadcasted_iota(jnp.int32, (rows, rows), 0)
-    i1 = lax.broadcasted_iota(jnp.int32, (rows, rows), 1)
     picked = ids_row == lax.broadcasted_iota(jnp.int32, (experts, rows), 0)
     gate = jax.nn.sigmoid(jnp.sum(jnp.where(picked, logits, 0.0), 0, keepdims=True))
-    running = jnp.dot(
-        picked.astype(F32).astype(BF16),
-        (i0 <= i1).astype(F32).astype(BF16),
-        preferred_element_type=F32,
-    )
-    rank = jnp.sum(jnp.where(picked, running, 0.0), 0, keepdims=True)
-    position = ids_row * SLOTS + rank.astype(jnp.int32) - 1
+    position = place_row[...]
     aux_row = lax.broadcasted_iota(jnp.int32, (128, rows), 0)
     aux[...] = jnp.where(aux_row == 0, gate, position.astype(F32)).T
     copies.append(pltpu.make_async_copy(aux, aux_ref, sems.at[5]))
@@ -185,43 +190,52 @@
 
 
 def second_half_kernel(
-    x_ref, normed_ref, m0, m1, o0, o1, ctx_ref, gain_ref, router_ref, row_ref,
+    x_ref, n_ref, m0, m1, o0, o1, ctx_ref, gain_ref, router_ref, row_ref, position_ref,
     att_ref, out_ref, aux_ref,
-    x, gain, router, ids, w, wo, ctx, projected, normed, sent, att, aux, sems, small,
+    x, gain, router, ids, place_row, w, wo, ctx, projected, normed, sent, att, aux, sems, small,
 ):
     core = my_core()
     qkv, late = fetch((o0, o1), 1 - core, w, sems.at[0], wo, sems.at[1])
     _, later = fetch((m0, m1), core, None, None, wo, sems.at[2])
     loads = start_all(
-        [(x_ref.at[0], x), (gain_ref, gain), (router_ref, router), (row_ref.at[0], ids)], small
+        [
+            (x_ref.at[0], x), (gain_ref, gain), (router_ref, router), (row_ref.at[0], ids),
+            (position_ref.at[0], place_row),
+        ],
+        small,
     )
     ctx[core] = ctx_ref[...]
     wait_all(qkv)
-    project(normed_ref, w.at[1 - core], projected)
+    project(n_ref, w.at[1 - core], projected)
 
     def store(pair, row, context):
         ctx[1 - core, row : row + context.shape[0], pair * 128 : pair * 128 + 128] = context
 
     attend(projected, store)
     wait_all(late + later + loads)
-    finish(x, ctx, wo, gain, router, ids, att_ref, out_ref, aux_ref, normed, sent, att, aux, small)
+    finish(
+        x, ctx, wo, gain, router, ids, place_row, att_ref, out_ref, aux_ref,
+        normed, sent, att, aux, small,
+    )
 
 
 def whole_kernel(
-    x_ref, gain1_ref, m0, m1, o0, o1, gain_ref, router_ref, row_ref,
+    x_ref, n_ref, m0, m1, o0, o1, gain_ref, router_ref, row_ref, position_ref,
     att_ref, out_ref, aux_ref,
-    gain1, x, gain, router, ids, w, wo, ctx, projected, normed, sent, att, aux, sems, small,
+    x, gain, router, ids, place_row, w, wo, ctx, projected, normed, sent, att, aux, sems, small,
 ):
     core = my_core()
-    first = start_all([(x_ref.at[1], x), (gain1_ref, gain1)], small)
+    first = start_all([(n_ref.at[1], normed)], small.at[pl.ds(5, 1)])
     qkv, late = fetch((m0, m1), core, w, sems.at[0], wo, sems.at[1])
     qkv2, late2 = fetch((o0, o1), 1 - core, w, sems.at[2], wo, sems.at[3])
     loads = start_all(
-        [(gain_ref, gain), (router_ref, router), (row_ref.at[1], ids)], small.at[pl.ds(2, 3)]
-    )
-    wait_all(first)
-    normed[...] = scale_rows(x[...], gain1[...]).astype(BF16)
-    wait_all(qkv + qkv2)
+        [
+            (x_ref.at[1], x), (gain_ref, gain), (router_ref, router), (row_ref.at[1], ids),
+            (position_ref.at[1], place_row),
+        ],
+        small,
+    )
+    wait_all(first + qkv + qkv2)
 
     def step(side, carry):
         def store(pair, row, context):
@@ -233,7 +247,10 @@
 
     lax.fori_loop(0, 2, step, 0)
     wait_all(late + late2 + loads)
-    finish(x, ctx, wo, gain, router, ids, att_ref, out_ref, aux_ref, normed, sent, att, aux, small)
+    finish(
+        x, ctx, wo, gain, router, ids, place_row, att_ref, out_ref, aux_ref,
+        normed, sent, att, aux, small,
+    )
 
 
 def expert_kernel(x_ref, in_ref, out_ref, y_ref, total, hidden):
@@ -314,14 +331,33 @@
     swap = [(i, i ^ 1) for i in range(128)]
     steps = (1, -1, 2)
     own = jnp.concatenate([piece] + [lax.ppermute(piece, ALL, hop(d, 0)) for d in steps], axis=0)
+    ids_row = expert_ids.reshape(batches, 1, rows)
+    normed, position = pl.pallas_call(
+        prepare_kernel,
+        grid=(batches,),
+        out_shape=(
+            jax.ShapeDtypeStruct((batches, rows, width), BF16),
+            jax.ShapeDtypeStruct((batches, 1, rows), jnp.int32),
+        ),
+        in_specs=[
+            pl.BlockSpec((1, rows, width), lambda b: (b, 0, 0)),
+            pl.BlockSpec((width,), lambda b: (0,)),
+            pl.BlockSpec((1, 1, rows), lambda b: (b, 0, 0)),
+        ],
+        out_specs=(
+            pl.BlockSpec((1, rows, width), lambda b: (b, 0, 0)),
+            pl.BlockSpec((1, 1, rows), lambda b: (b, 0, 0)),
+        ),
+        compiler_params=limit(47104),
+        name="prepare",
+    )(tokens, norm_attn, ids_row)
+    own, normed, position = lax.optimization_barrier((own, normed, position))
     rest = jnp.concatenate([lax.ppermute(own, ALL, hop(d, 1)) for d in steps], axis=0)
     mine = [own, rest]
     other = [lax.ppermute(part, ALL, swap) for part in mine]
     mine = [pltpu.with_memory_space_constraint(part, pltpu.VMEM) for part in mine]
     other = [pltpu.with_memory_space_constraint(part, pltpu.VMEM) for part in other]
 
-    ids_row = expert_ids.reshape(batches, 1, rows)
-
     any_spec = pl.BlockSpec(memory_space=pltpu.HBM)
     whole = pl.BlockSpec(memory_space=pltpu.VMEM)
 
@@ -335,25 +371,23 @@
     projected = pltpu.VMEM((rows, 3 * HALF), BF16)
     one = pltpu.VMEM((rows, width), BF16)
     gain_scratch = pltpu.VMEM((width,), F32)
-    ctx_mine, normed = pl.pallas_call(
+    ctx_mine, normed_first = pl.pallas_call(
         context_kernel,
         out_shape=(
             jax.ShapeDtypeStruct((rows, HALF), BF16),
             jax.ShapeDtypeStruct((rows, width), BF16),
         ),
-        in_specs=[any_spec] * 2 + [whole] * 2,
+        in_specs=[any_spec] + [whole] * 2,
         out_specs=(whole, whole),
         scratch_shapes=[
-            one,
-            gain_scratch,
             w_scratch,
             projected,
             pltpu.SemaphoreType.DMA((16,)),
-            pltpu.SemaphoreType.DMA((2,)),
+            pltpu.SemaphoreType.DMA((1,)),
         ],
         compiler_params=limit(47104),
         name="first_half",
-    )(tokens, norm_attn, *mine)
+    )(normed, *mine)
 
     finish_out = (
         jax.ShapeDtypeStruct((rows, width), BF16),
@@ -365,6 +399,7 @@
         one,
         gain_scratch,
         pltpu.VMEM((width, experts), BF16),
+        pltpu.VMEM((1, rows), jnp.int32),
         pltpu.VMEM((1, rows), jnp.int32),
         w_scratch,
         pltpu.VMEM((width, width), BF16),
@@ -381,22 +416,22 @@
     first = pl.pallas_call(
         second_half_kernel,
         out_shape=finish_out,
-        in_specs=[any_spec] + [whole] * 6 + [any_spec] * 3,
+        in_specs=[any_spec] + [whole] * 6 + [any_spec] * 4,
         out_specs=finish_specs,
         scratch_shapes=scratch,
         compiler_params=limit(54000),
         name="second_half",
-    )(tokens, near(normed), *mine, *other, near(ctx_mine), norm_ffn, router, ids_row)
+    )(tokens, near(normed_first), *mine, *other, near(ctx_mine), norm_ffn, router, ids_row, position)
 
     second = pl.pallas_call(
         whole_kernel,
         out_shape=finish_out,
-        in_specs=[any_spec] * 2 + [whole] * 4 + [any_spec] * 3,
+        in_specs=[any_spec] * 2 + [whole] * 4 + [any_spec] * 4,
         out_specs=finish_specs,
-        scratch_shapes=[gain_scratch] + scratch,
+        scratch_shapes=scratch,
         compiler_params=limit(54000),
         name="whole",
-    )(tokens, norm_attn, *mine, *other, norm_ffn, router, ids_row)
+    )(tokens, normed, *mine, *other, norm_ffn, router, ids_row, position)
 
     def exchange(values):
         moved = lax.all_to_all(values, ALL, split_axis=0, concat_axis=0, tiled=True)

time: 169 us -> 169 us (level)
  waiting for transfers between devices: 71 us -> 67.9 us
  local copies, waits for them, and re-layouts: 2.55 us -> 5.31 us
    ppermute x3, waiting for transfers between devices: 4.57 us -> 0.92 us  [body(): lax.ppermute(piece, ALL, hop(d, 0))]
    unnamed x18 -> x16, local copies, waits for them, and re-layouts: 1.59 us -> 4.34 us
  transfers between devices with their start and end apart: 12 -> 12, of which waited for: 9 -> 8; matrix products, arithmetic and copies ran while one was open for 0% -> 0% of each run, Pallas kernels for 29% -> 29%
where the time goes in v2:
time: 169 us; the launch traced here: 168 us
  waiting for transfers between devices  67.9 us (40%)
  Pallas kernels  59.3 us (35%)
  starting transfers between devices  35 us (21%)
  local copies, waits for them, and re-layouts  5.31 us (3%)
    all_to_all x4, waiting for transfers between devices, exchange(): moved = lax.all_to_all(values, ALL, split_axis=0, concat_axis=0, tiled=True)  53.8 us
    pallas_call x2, Pallas kernels, serve(): pl.pallas_call(expert_kernel, grid=(hidden // chunk,), out_shape=jax.Shap...  28.2 us
    all_to_all x4, starting transfers between devices, exchange(): moved = lax.all_to_all(values, ALL, split_axis=0, concat_axis=0, tiled=True)  21.4 us
    ppermute x3, waiting for transfers between devices, body(): lax.ppermute(own, ALL, hop(d, 1))  13.2 us
    pallas_call x1, Pallas kernels, body(): pl.pallas_call(whole_kernel, out_shape=finish_out, in_specs=[any_spec] *...  11.9 us
    pallas_call x1, Pallas kernels, body(): pl.pallas_call(second_half_kernel, out_shape=finish_out, in_specs=[any_sp...  8.07 us
    ppermute x3, starting transfers between devices, body(): lax.ppermute(piece, ALL, hop(d, 0))  5.95 us
    unnamed x16, local copies, waits for them, and re-layouts  4.34 us
  transfers between devices with their start and end apart: 12, of which 8 were waited for; matrix products, arithmetic and copies ran while one was open for 0% of the time, Pallas kernels for 29%

profile of v2, /device:TPU:1, one launch (start us, length us, event | category | flops | bytes accessed | tf_op | source)
XLA Modules:
  0.0 168.0 jit_solution(4420147760770128136)
XLA Ops:
  0.0 0.9 fusion
  1.0 2.5 %collective-permute-start = (bf16[48,1536]{1,0:T(8,128)(2,1)S(1)}, bf16[48,1536]{1,0:T(8,128)(2,1)S(1)}, u32[]{:S(2)}, u32[]{:S(2)}) collective-permute-start(bf16[48,1536]{1,0:T(8,128)(2,1)S(1)} %maximum_select_fusion), channel_id=1, source_target_pairs={{0,32},{1,9},{2,34},{3,11},{4,36},{5,13},{6,38},{7,15},{8,40},{9,1... | collective-permute-start | bytes 442376 | tf_op jit(solution)/shard_map/ppermute | solution.py:333
  3.5 2.2 %collective-permute-start.1 = (bf16[48,1536]{1,0:T(8,128)(2,1)S(1)}, bf16[48,1536]{1,0:T(8,128)(2,1)S(1)}, u32[]{:S(2)}, u32[]{:S(2)}) collective-permute-start(bf16[48,1536]{1,0:T(8,128)(2,1)S(1)} %maximum_select_fusion), channel_id=1, source_target_pairs={{0,96},{1,25},{2,98},{3,27},{4,100},{5,29},{6,102},{7,31},{8,104},... | collective-permute-start | bytes 442376 | tf_op jit(solution)/shard_map/ppermute | solution.py:333
  5.7 1.2 collective-permute-start.2
  6.9 1.4 copy-done
  8.3 0.7 copy-done.4
  9.0 0.7 copy-done.6
  9.7 0.8 prepare.1
  10.6 0.9 collective-permute-done.2
  11.5 1.0 collective-permute-start.3
  12.5 1.8 %collective-permute-start.4 = (bf16[192,1536]{1,0:T(8,128)(2,1)S(1)}, bf16[192,1536]{1,0:T(8,128)(2,1)S(1)}, u32[]{:S(2)}, u32[]{:S(2)}) collective-permute-start(bf16[192,1536]{1,0:T(8,128)(2,1)S(1)} %pad_maximum_fusion.m0.b0), channel_id=1, source_target_pairs={{0,24},{1,97},{2,26},{3,99},{4,28},{5,101},{6,30},{7,103},{8,0},{9... | collective-permute-start | bytes 1769480 | tf_op jit(solution)/shard_map/ppermute | solution.py:355
  14.3 1.2 collective-permute-start.5
  15.5 6.3 %collective-permute-done.3 = bf16[192,1536]{1,0:T(8,128)(2,1)S(1)} collective-permute-done((bf16[192,1536]{1,0:T(8,128)(2,1)S(1)}, bf16[192,1536]{1,0:T(8,128)(2,1)S(1)}, u32[]{:S(2)}, u32[]{:S(2)}) %collective-permute-start.3) | collective-permute-done | bytes 589856 | tf_op jit(solution)/shard_map/ppermute | solution.py:355
  21.9 5.5 %collective-permute-done.4 = bf16[192,1536]{1,0:T(8,128)(2,1)S(1)} collective-permute-done((bf16[192,1536]{1,0:T(8,128)(2,1)S(1)}, bf16[192,1536]{1,0:T(8,128)(2,1)S(1)}, u32[]{:S(2)}, u32[]{:S(2)}) %collective-permute-start.4) | collective-permute-done | bytes 589856 | tf_op jit(solution)/shard_map/ppermute | solution.py:355
  27.5 1.4 collective-permute-done.5
  28.9 3.4 %collective-permute-start.7 = (bf16[576,1536]{1,0:T(8,128)(2,1)S(1)}, bf16[576,1536]{1,0:T(8,128)(2,1)S(1)}, u32[]{:S(2)}, u32[]{:S(2)}) collective-permute-start(bf16[576,1536]{1,0:T(8,128)(2,1)S(1)} %constant_dynamic-update-slice_fusion.m1.b1), channel_id=1, source_target_pairs={{0,1},{1,0},{2,3},{3,2},{4,5},{5,4},{6,7},{7,6},{8,9},{9,8},{10,11... | collective-permute-start | bytes 5308424 | tf_op jit(solution)/shard_map/ppermute | solution.py:357
  32.6 4.2 %first_half.1 = (bf16[512,384]{1,0:T(8,128)(2,1)S(1)}, bf16[512,768]{1,0:T(8,128)(2,1)S(1)}) custom-call(bf16[2,512,768]{2,1,0:T(8,128)(2,1)S(1)} %get-tuple-element.20.n_ref, bf16[192,1536]{1,0:T(8,128)(2,1)S(1)} %pad_maximum_fusion.m0.b0, bf16[576,1536]{1,0:T(8,128)(2,1)S(1)} %constant_dynamic-update-slice_fusion.m1.b1), custom_call_target="tpu_custom_call" | custom-call | tf_op jit(solution)/shard_map/first_half/pallas_call | solution.py:374
  36.8 8.1 %second_half.1 = (bf16[512,768]{1,0:T(8,128)(2,1)}, bf16[128,8,768]{2,1,0:T(8,128)(2,1)}, f32[512,128]{1,0:T(8,128)}) custom-call(bf16[2,512,768]{2,1,0:T(8,128)(2,1)} %x_ref.5, bf16[512,768]{1,0:T(8,128)(2,1)S(1)} %get-tuple-element.26.n_ref, bf16[192,1536]{1,0:T(8,128)(2,1)S(1)} %pad_maximum_fusion.m0.b0, ...), custom_call_target="tpu_custom_call" | custom-call | tf_op jit(solution)/shard_map/second_half/pallas_call | solution.py:416
  44.9 7.3 %all-to-all-start.2 = ((bf16[128,8,768]{2,1,0:T(8,128)(2,1)}), bf16[128,8,768]{2,1,0:T(8,128)(2,1)}, u32[]{:S(2)}, u32[]{:S(2)}) async-start(bf16[128,8,768]{2,1,0:T(8,128)(2,1)} %get-tuple-element.30), calls=%async_computation.2 | async-start | bytes 3145728 | tf_op jit(solution)/shard_map/all_to_all | solution.py:437
  52.2 1.5 copy-done.2
  53.7 11.9 %whole.1 = (bf16[512,768]{1,0:T(8,128)(2,1)}, bf16[128,8,768]{2,1,0:T(8,128)(2,1)}, f32[512,128]{1,0:T(8,128)}) custom-call(bf16[2,512,768]{2,1,0:T(8,128)(2,1)} %x_ref.5, bf16[2,512,768]{2,1,0:T(8,128)(2,1)} %copy-done.3, bf16[192,1536]{1,0:T(8,128)(2,1)S(1)} %pad_maximum_fusion.m0.b0, bf16[576,1536]{1,0:T(8,128)(2,1)S(1)} %constant_dynamic-update-slice_fusion.m1.b1, ...), custom_call_target="tpu_custom_call" | custom-call | tf_op jit(solution)/shard_map/whole/pallas_call | solution.py:426
  65.6 10.9 %all-to-all-done.2.x_ref = bf16[128,8,768]{2,1,0:T(8,128)(2,1)} async-done(((bf16[128,8,768]{2,1,0:T(8,128)(2,1)}), bf16[128,8,768]{2,1,0:T(8,128)(2,1)}, u32[]{:S(2)}, u32[]{:S(2)}) %all-to-all-start.2) | async-done | bytes 1572896 | tf_op jit(solution)/shard_map/all_to_all | solution.py:437
  76.5 4.7 %all-to-all-start = ((bf16[128,8,768]{2,1,0:T(8,128)(2,1)}), bf16[128,8,768]{2,1,0:T(8,128)(2,1)S(1)}, u32[]{:S(2)}, u32[]{:S(2)}) async-start(bf16[128,8,768]{2,1,0:T(8,128)(2,1)} %get-tuple-element.25), calls=%async_computation | async-start | bytes 3145728 | tf_op jit(solution)/shard_map/all_to_all | solution.py:437
  81.2 14.3 %expert.3 = bf16[128,8,768]{2,1,0:T(8,128)(2,1)} custom-call(bf16[128,8,768]{2,1,0:T(8,128)(2,1)} %all-to-all-done.2.x_ref, bf16[1,768,3072]{2,1,0:T(8,128)(2,1)} %in_ref.3, bf16[1,3072,768]{2,1,0:T(8,128)(2,1)} %out_ref.3), custom_call_target="tpu_custom_call" | custom-call | tf_op jit(solution)/shard_map/expert/pallas_call | solution.py:443
  95.5 10.4 %all-to-all-done.x_ref = bf16[128,8,768]{2,1,0:T(8,128)(2,1)S(1)} async-done(((bf16[128,8,768]{2,1,0:T(8,128)(2,1)}), bf16[128,8,768]{2,1,0:T(8,128)(2,1)S(1)}, u32[]{:S(2)}, u32[]{:S(2)}) %all-to-all-start) | async-done | bytes 1572896 | tf_op jit(solution)/shard_map/all_to_all | solution.py:437
  105.9 4.7 %all-to-all-start.3 = ((bf16[128,8,768]{2,1,0:T(8,128)(2,1)}), bf16[128,8,768]{2,1,0:T(8,128)(2,1)S(1)}, u32[]{:S(2)}, u32[]{:S(2)}) async-start(bf16[128,8,768]{2,1,0:T(8,128)(2,1)} %expert.3), calls=%async_computation.3 | async-start | bytes 3145728 | tf_op jit(solution)/shard_map/all_to_all | solution.py:437
  110.6 13.8 %expert.2 = bf16[128,8,768]{2,1,0:T(8,128)(2,1)} custom-call(bf16[128,8,768]{2,1,0:T(8,128)(2,1)S(1)} %all-to-all-done.x_ref, bf16[1,768,3072]{2,1,0:T(8,128)(2,1)} %in_ref.3, bf16[1,3072,768]{2,1,0:T(8,128)(2,1)} %out_ref.3), custom_call_target="tpu_custom_call" | custom-call | tf_op jit(solution)/shard_map/expert/pallas_call | solution.py:443
  124.4 10.9 %all-to-all-done.3.back_ref = bf16[128,8,768]{2,1,0:T(8,128)(2,1)S(1)} async-done(((bf16[128,8,768]{2,1,0:T(8,128)(2,1)}), bf16[128,8,768]{2,1,0:T(8,128)(2,1)S(1)}, u32[]{:S(2)}, u32[]{:S(2)}) %all-to-all-start.3) | async-done | bytes 1572896 | tf_op jit(solution)/shard_map/all_to_all | solution.py:437
  135.3 4.7 %all-to-all-start.1 = ((bf16[128,8,768]{2,1,0:T(8,128)(2,1)}), bf16[128,8,768]{2,1,0:T(8,128)(2,1)S(1)}, u32[]{:S(2)}, u32[]{:S(2)}) async-start(bf16[128,8,768]{2,1,0:T(8,128)(2,1)} %expert.2), calls=%async_computation.1 | async-start | bytes 3145728 | tf_op jit(solution)/shard_map/all_to_all | solution.py:437
  140.0 3.1 %combine0.1.held_ref = bf16[2,512,768]{2,1,0:T(8,128)(2,1)} custom-call(bf16[512,768]{1,0:T(8,128)(2,1)} %get-tuple-element.28.att_ref, f32[512,128]{1,0:T(8,128)} %get-tuple-element.29.aux_ref, bf16[128,8,768]{2,1,0:T(8,128)(2,1)S(1)} %all-to-all-done.3.back_ref), custom_call_target="tpu_custom_call" | custom-call | tf_op jit(solution)/shard_map/combine0/pallas_call | solution.py:468
  143.1 21.6 %all-to-all-done.1.back_ref = bf16[128,8,768]{2,1,0:T(8,128)(2,1)S(1)} async-done(((bf16[128,8,768]{2,1,0:T(8,128)(2,1)}), bf16[128,8,768]{2,1,0:T(8,128)(2,1)S(1)}, u32[]{:S(2)}, u32[]{:S(2)}) %all-to-all-start.1) | async-done | bytes 1572896 | tf_op jit(solution)/shard_map/all_to_all | solution.py:437
  164.7 3.1 %combine1.1 = bf16[2,512,768]{2,1,0:T(8,128)(2,1)} custom-call(bf16[512,768]{1,0:T(8,128)(2,1)} %get-tuple-element.23.att_ref, f32[512,128]{1,0:T(8,128)} %get-tuple-element.24.aux_ref, bf16[128,8,768]{2,1,0:T(8,128)(2,1)S(1)} %all-to-all-done.1.back_ref, bf16[2,512,768]{2,1,0:T(8,128)(2,1)} %combine0.1.held_ref), custom_call_target="tpu_custom_call", output_to_operand_aliasing={{}: (3, {})} | custom-call | tf_op jit(solution)/shard_map/combine1/pallas_call | solution.py:477
  (20 shorter events, 0.5 us)
Async XLA Ops:
  1.0 9.6 %collective-permute-start = (bf16[48,1536]{1,0:T(8,128)(2,1)S(1)}, bf16[48,1536]{1,0:T(8,128)(2,1)S(1)}, u32[]{:S(2)}, u32[]{:S(2)}) collective-permute-start(bf16[48,1536]{1,0:T(8,128)(2,1)S(1)} %maximum_select_fusion), channel_id=1, source_target_pairs={{0,32},{1,9},{2,34},{3,11},{4,36},{5,13},{6,38},{7,15},{8,40},{9,1... | collective-permute-start | bytes 442376 | tf_op jit(solution)/shard_map/ppermute | solution.py:333
  3.5 7.1 %collective-permute-start.1 = (bf16[48,1536]{1,0:T(8,128)(2,1)S(1)}, bf16[48,1536]{1,0:T(8,128)(2,1)S(1)}, u32[]{:S(2)}, u32[]{:S(2)}) collective-permute-start(bf16[48,1536]{1,0:T(8,128)(2,1)S(1)} %maximum_select_fusion), channel_id=1, source_target_pairs={{0,96},{1,25},{2,98},{3,27},{4,100},{5,29},{6,102},{7,31},{8,104},... | collective-permute-start | bytes 442376 | tf_op jit(solution)/shard_map/ppermute | solution.py:333
  5.7 5.8 %collective-permute-start.2 = (bf16[48,1536]{1,0:T(8,128)(2,1)S(1)}, bf16[48,1536]{1,0:T(8,128)(2,1)S(1)}, u32[]{:S(2)}, u32[]{:S(2)}) collective-permute-start(bf16[48,1536]{1,0:T(8,128)(2,1)S(1)} %maximum_select_fusion), channel_id=1, source_target_pairs={{0,64},{1,17},{2,66},{3,19},{4,68},{5,21},{6,70},{7,23},{8,72},{9,... | collective-permute-start | bytes 442376 | tf_op jit(solution)/shard_map/ppermute | solution.py:333
  6.9 1.4 copy-start
  8.3 0.7 copy-start.4
  9.0 0.7 copy-start.6
  10.5 16.9 %copy-start.5 = (s32[2,1,512]{2,1,0:T(1,128)}, s32[2,1,512]{2,1,0:T(1,128)S(1)}, u32[]{:S(2)}) copy-start(s32[2,1,512]{2,1,0:T(1,128)S(1)} %get-tuple-element.22.position_ref) | copy-start | bytes 12292
  10.6 22.1 %copy-start.3 = (bf16[2,512,768]{2,1,0:T(8,128)(2,1)}, bf16[2,512,768]{2,1,0:T(8,128)(2,1)S(1)}, u32[]{:S(2)}) copy-start(bf16[2,512,768]{2,1,0:T(8,128)(2,1)S(1)} %get-tuple-element.20.n_ref) | copy-start | bytes 4718596
  11.5 10.3 %collective-permute-start.3 = (bf16[192,1536]{1,0:T(8,128)(2,1)S(1)}, bf16[192,1536]{1,0:T(8,128)(2,1)S(1)}, u32[]{:S(2)}, u32[]{:S(2)}) collective-permute-start(bf16[192,1536]{1,0:T(8,128)(2,1)S(1)} %pad_maximum_fusion.m0.b0), channel_id=1, source_target_pairs={{0,8},{1,33},{2,10},{3,35},{4,12},{5,37},{6,14},{7,39},{8,16},{9,4... | collective-permute-start | bytes 1769480 | tf_op jit(solution)/shard_map/ppermute | solution.py:355
  12.5 14.9 %collective-permute-start.4 = (bf16[192,1536]{1,0:T(8,128)(2,1)S(1)}, bf16[192,1536]{1,0:T(8,128)(2,1)S(1)}, u32[]{:S(2)}, u32[]{:S(2)}) collective-permute-start(bf16[192,1536]{1,0:T(8,128)(2,1)S(1)} %pad_maximum_fusion.m0.b0), channel_id=1, source_target_pairs={{0,24},{1,97},{2,26},{3,99},{4,28},{5,101},{6,30},{7,103},{8,0},{9... | collective-permute-start | bytes 1769480 | tf_op jit(solution)/shard_map/ppermute | solution.py:355
  14.3 14.6 %collective-permute-start.5 = (bf16[192,1536]{1,0:T(8,128)(2,1)S(1)}, bf16[192,1536]{1,0:T(8,128)(2,1)S(1)}, u32[]{:S(2)}, u32[]{:S(2)}) collective-permute-start(bf16[192,1536]{1,0:T(8,128)(2,1)S(1)} %pad_maximum_fusion.m0.b0), channel_id=1, source_target_pairs={{0,16},{1,65},{2,18},{3,67},{4,20},{5,69},{6,22},{7,71},{8,24},{9,... | collective-permute-start | bytes 1769480 | tf_op jit(solution)/shard_map/ppermute | solution.py:355
  28.9 7.9 %collective-permute-start.7 = (bf16[576,1536]{1,0:T(8,128)(2,1)S(1)}, bf16[576,1536]{1,0:T(8,128)(2,1)S(1)}, u32[]{:S(2)}, u32[]{:S(2)}) collective-permute-start(bf16[576,1536]{1,0:T(8,128)(2,1)S(1)} %constant_dynamic-update-slice_fusion.m1.b1), channel_id=1, source_target_pairs={{0,1},{1,0},{2,3},{3,2},{4,5},{5,4},{6,7},{7,6},{8,9},{9,8},{10,11... | collective-permute-start | bytes 5308424 | tf_op jit(solution)/shard_map/ppermute | solution.py:357
  32.3 4.4 %collective-permute-start.6 = (bf16[192,1536]{1,0:T(8,128)(2,1)S(1)}, bf16[192,1536]{1,0:T(8,128)(2,1)S(1)}, u32[]{:S(2)}, u32[]{:S(2)}) collective-permute-start(bf16[192,1536]{1,0:T(8,128)(2,1)S(1)} %pad_maximum_fusion.m0.b0), channel_id=1, source_target_pairs={{0,1},{1,0},{2,3},{3,2},{4,5},{5,4},{6,7},{7,6},{8,9},{9,8},{10,11... | collective-permute-start | bytes 1769480 | tf_op jit(solution)/shard_map/ppermute | solution.py:357
  36.8 8.1 %copy-start.1 = (bf16[576,1536]{1,0:T(8,128)(2,1)}, bf16[576,1536]{1,0:T(8,128)(2,1)S(1)}, u32[]{:S(2)}) copy-start(bf16[576,1536]{1,0:T(8,128)(2,1)S(1)} %collective-permute-done.7.o1) | copy-start | bytes 5308420
  44.9 31.6 %all-to-all-start.2 = ((bf16[128,8,768]{2,1,0:T(8,128)(2,1)}), bf16[128,8,768]{2,1,0:T(8,128)(2,1)}, u32[]{:S(2)}, u32[]{:S(2)}) async-start(bf16[128,8,768]{2,1,0:T(8,128)(2,1)} %get-tuple-element.30), calls=%async_computation.2 | async-start | bytes 3145728 | tf_op jit(solution)/shard_map/all_to_all | solution.py:437
  52.2 1.5 copy-start.2
  76.5 29.4 %all-to-all-start = ((bf16[128,8,768]{2,1,0:T(8,128)(2,1)}), bf16[128,8,768]{2,1,0:T(8,128)(2,1)S(1)}, u32[]{:S(2)}, u32[]{:S(2)}) async-start(bf16[128,8,768]{2,1,0:T(8,128)(2,1)} %get-tuple-element.25), calls=%async_computation | async-start | bytes 3145728 | tf_op jit(solution)/shard_map/all_to_all | solution.py:437
  105.9 29.4 %all-to-all-start.3 = ((bf16[128,8,768]{2,1,0:T(8,128)(2,1)}), bf16[128,8,768]{2,1,0:T(8,128)(2,1)S(1)}, u32[]{:S(2)}, u32[]{:S(2)}) async-start(bf16[128,8,768]{2,1,0:T(8,128)(2,1)} %expert.3), calls=%async_computation.3 | async-start | bytes 3145728 | tf_op jit(solution)/shard_map/all_to_all | solution.py:437
  135.3 29.4 %all-to-all-start.1 = ((bf16[128,8,768]{2,1,0:T(8,128)(2,1)}), bf16[128,8,768]{2,1,0:T(8,128)(2,1)S(1)}, u32[]{:S(2)}, u32[]{:S(2)}) async-start(bf16[128,8,768]{2,1,0:T(8,128)(2,1)} %expert.2), calls=%async_computation.1 | async-start | bytes 3145728 | tf_op jit(solution)/shard_map/all_to_all | solution.py:437

commit v3 on v2

--- a/solution.py
+++ b/solution.py
@@ -163,17 +163,7 @@
         normed[mine] = scale_rows(attended, gain[...]).astype(BF16)
     copies = [pltpu.make_async_copy(att, att_ref, sems.at[4])]
     copies[0].start()
-    ids_row = ids[...]
-    logits = lax.dot_general(
-        router[...], normed[...], (((0,), (1,)), ((), ())), preferred_element_type=F32
-    )
-    picked = ids_row == lax.broadcasted_iota(jnp.int32, (experts, rows), 0)
-    gate = jax.nn.sigmoid(jnp.sum(jnp.where(picked, logits, 0.0), 0, keepdims=True))
     position = place_row[...]
-    aux_row = lax.broadcasted_iota(jnp.int32, (128, rows), 0)
-    aux[...] = jnp.where(aux_row == 0, gate, position.astype(F32)).T
-    copies.append(pltpu.make_async_copy(aux, aux_ref, sems.at[5]))
-    copies[1].start()
     for slot in range(0, experts * SLOTS, block):
         number = lax.broadcasted_iota(jnp.int32, (block, rows), 0) + slot
         spread = (number == position).astype(F32).astype(BF16)
@@ -186,6 +176,16 @@
         copy = pltpu.make_async_copy(sent.at[some], out_ref.at[some], sems.at[slot // block])
         copy.start()
         copies.append(copy)
+    ids_row = ids[...]
+    logits = lax.dot_general(
+        router[...], normed[...], (((0,), (1,)), ((), ())), preferred_element_type=F32
+    )
+    picked = ids_row == lax.broadcasted_iota(jnp.int32, (experts, rows), 0)
+    gate = jax.nn.sigmoid(jnp.sum(jnp.where(picked, logits, 0.0), 0, keepdims=True))
+    aux_row = lax.broadcasted_iota(jnp.int32, (128, rows), 0)
+    aux[...] = jnp.where(aux_row == 0, gate, position.astype(F32)).T
+    copies.append(pltpu.make_async_copy(aux, aux_ref, sems.at[5]))
+    copies[-1].start()
     wait_all(copies)
 
 

time: 169 us -> 169 us (level)
  no operation moved by 1% of the time
where the time goes in v3:
time: 169 us; the launch traced here: 168 us
  waiting for transfers between devices  67.9 us (40%)
  Pallas kernels  59.4 us (35%)
  starting transfers between devices  35 us (21%)
  local copies, waits for them, and re-layouts  5.31 us (3%)
    all_to_all x4, waiting for transfers between devices, exchange(): moved = lax.all_to_all(values, ALL, split_axis=0, concat_axis=0, tiled=True)  53.8 us
    pallas_call x2, Pallas kernels, serve(): pl.pallas_call(expert_kernel, grid=(hidden // chunk,), out_shape=jax.Shap...  28.2 us
    all_to_all x4, starting transfers between devices, exchange(): moved = lax.all_to_all(values, ALL, split_axis=0, concat_axis=0, tiled=True)  21.4 us
    ppermute x3, waiting for transfers between devices, body(): lax.ppermute(own, ALL, hop(d, 1))  13.2 us
    pallas_call x1, Pallas kernels, body(): pl.pallas_call(whole_kernel, out_shape=finish_out, in_specs=[any_spec] *...  11.9 us
    pallas_call x1, Pallas kernels, body(): pl.pallas_call(second_half_kernel, out_shape=finish_out, in_specs=[any_sp...  8.14 us
    ppermute x3, starting transfers between devices, body(): lax.ppermute(piece, ALL, hop(d, 0))  5.95 us
    unnamed x16, local copies, waits for them, and re-layouts  4.34 us
  transfers between devices with their start and end apart: 12, of which 8 were waited for; matrix products, arithmetic and copies ran while one was open for 0% of the time, Pallas kernels for 29%

profile of v3, /device:TPU:1, one launch (start us, length us, event | category | flops | bytes accessed | tf_op | source)
XLA Modules:
  0.0 168.1 jit_solution(8432758966007685518)
XLA Ops:
  0.0 0.9 fusion
  1.0 2.5 %collective-permute-start = (bf16[48,1536]{1,0:T(8,128)(2,1)S(1)}, bf16[48,1536]{1,0:T(8,128)(2,1)S(1)}, u32[]{:S(2)}, u32[]{:S(2)}) collective-permute-start(bf16[48,1536]{1,0:T(8,128)(2,1)S(1)} %maximum_select_fusion), channel_id=1, source_target_pairs={{0,32},{1,9},{2,34},{3,11},{4,36},{5,13},{6,38},{7,15},{8,40},{9,1... | collective-permute-start | bytes 442376 | tf_op jit(solution)/shard_map/ppermute | solution.py:333
  3.5 2.2 %collective-permute-start.1 = (bf16[48,1536]{1,0:T(8,128)(2,1)S(1)}, bf16[48,1536]{1,0:T(8,128)(2,1)S(1)}, u32[]{:S(2)}, u32[]{:S(2)}) collective-permute-start(bf16[48,1536]{1,0:T(8,128)(2,1)S(1)} %maximum_select_fusion), channel_id=1, source_target_pairs={{0,96},{1,25},{2,98},{3,27},{4,100},{5,29},{6,102},{7,31},{8,104},... | collective-permute-start | bytes 442376 | tf_op jit(solution)/shard_map/ppermute | solution.py:333
  5.7 1.2 collective-permute-start.2
  6.9 1.4 copy-done
  8.3 0.7 copy-done.4
  9.0 0.7 copy-done.6
  9.7 0.8 prepare.1
  10.6 0.9 collective-permute-done.2
  11.5 1.0 collective-permute-start.3
  12.5 1.8 %collective-permute-start.4 = (bf16[192,1536]{1,0:T(8,128)(2,1)S(1)}, bf16[192,1536]{1,0:T(8,128)(2,1)S(1)}, u32[]{:S(2)}, u32[]{:S(2)}) collective-permute-start(bf16[192,1536]{1,0:T(8,128)(2,1)S(1)} %pad_maximum_fusion.m0.b0), channel_id=1, source_target_pairs={{0,24},{1,97},{2,26},{3,99},{4,28},{5,101},{6,30},{7,103},{8,0},{9... | collective-permute-start | bytes 1769480 | tf_op jit(solution)/shard_map/ppermute | solution.py:355
  14.3 1.2 collective-permute-start.5
  15.5 6.3 %collective-permute-done.3 = bf16[192,1536]{1,0:T(8,128)(2,1)S(1)} collective-permute-done((bf16[192,1536]{1,0:T(8,128)(2,1)S(1)}, bf16[192,1536]{1,0:T(8,128)(2,1)S(1)}, u32[]{:S(2)}, u32[]{:S(2)}) %collective-permute-start.3) | collective-permute-done | bytes 589856 | tf_op jit(solution)/shard_map/ppermute | solution.py:355
  21.9 5.5 %collective-permute-done.4 = bf16[192,1536]{1,0:T(8,128)(2,1)S(1)} collective-permute-done((bf16[192,1536]{1,0:T(8,128)(2,1)S(1)}, bf16[192,1536]{1,0:T(8,128)(2,1)S(1)}, u32[]{:S(2)}, u32[]{:S(2)}) %collective-permute-start.4) | collective-permute-done | bytes 589856 | tf_op jit(solution)/shard_map/ppermute | solution.py:355
  27.5 1.4 collective-permute-done.5
  28.9 3.4 %collective-permute-start.7 = (bf16[576,1536]{1,0:T(8,128)(2,1)S(1)}, bf16[576,1536]{1,0:T(8,128)(2,1)S(1)}, u32[]{:S(2)}, u32[]{:S(2)}) collective-permute-start(bf16[576,1536]{1,0:T(8,128)(2,1)S(1)} %constant_dynamic-update-slice_fusion.m1.b1), channel_id=1, source_target_pairs={{0,1},{1,0},{2,3},{3,2},{4,5},{5,4},{6,7},{7,6},{8,9},{9,8},{10,11... | collective-permute-start | bytes 5308424 | tf_op jit(solution)/shard_map/ppermute | solution.py:357
  32.6 4.2 %first_half.1 = (bf16[512,384]{1,0:T(8,128)(2,1)S(1)}, bf16[512,768]{1,0:T(8,128)(2,1)S(1)}) custom-call(bf16[2,512,768]{2,1,0:T(8,128)(2,1)S(1)} %get-tuple-element.20.n_ref, bf16[192,1536]{1,0:T(8,128)(2,1)S(1)} %pad_maximum_fusion.m0.b0, bf16[576,1536]{1,0:T(8,128)(2,1)S(1)} %constant_dynamic-update-slice_fusion.m1.b1), custom_call_target="tpu_custom_call" | custom-call | tf_op jit(solution)/shard_map/first_half/pallas_call | solution.py:374
  36.8 8.1 %second_half.1 = (bf16[512,768]{1,0:T(8,128)(2,1)}, bf16[128,8,768]{2,1,0:T(8,128)(2,1)}, f32[512,128]{1,0:T(8,128)}) custom-call(bf16[2,512,768]{2,1,0:T(8,128)(2,1)} %x_ref.5, bf16[512,768]{1,0:T(8,128)(2,1)S(1)} %get-tuple-element.26.n_ref, bf16[192,1536]{1,0:T(8,128)(2,1)S(1)} %pad_maximum_fusion.m0.b0, ...), custom_call_target="tpu_custom_call" | custom-call | tf_op jit(solution)/shard_map/second_half/pallas_call | solution.py:416
  45.0 7.3 %all-to-all-start.2 = ((bf16[128,8,768]{2,1,0:T(8,128)(2,1)}), bf16[128,8,768]{2,1,0:T(8,128)(2,1)}, u32[]{:S(2)}, u32[]{:S(2)}) async-start(bf16[128,8,768]{2,1,0:T(8,128)(2,1)} %get-tuple-element.30), calls=%async_computation.2 | async-start | bytes 3145728 | tf_op jit(solution)/shard_map/all_to_all | solution.py:437
  52.3 1.5 copy-done.2
  53.8 11.9 %whole.1 = (bf16[512,768]{1,0:T(8,128)(2,1)}, bf16[128,8,768]{2,1,0:T(8,128)(2,1)}, f32[512,128]{1,0:T(8,128)}) custom-call(bf16[2,512,768]{2,1,0:T(8,128)(2,1)} %x_ref.5, bf16[2,512,768]{2,1,0:T(8,128)(2,1)} %copy-done.3, bf16[192,1536]{1,0:T(8,128)(2,1)S(1)} %pad_maximum_fusion.m0.b0, bf16[576,1536]{1,0:T(8,128)(2,1)S(1)} %constant_dynamic-update-slice_fusion.m1.b1, ...), custom_call_target="tpu_custom_call" | custom-call | tf_op jit(solution)/shard_map/whole/pallas_call | solution.py:426
  65.7 10.9 %all-to-all-done.2.x_ref = bf16[128,8,768]{2,1,0:T(8,128)(2,1)} async-done(((bf16[128,8,768]{2,1,0:T(8,128)(2,1)}), bf16[128,8,768]{2,1,0:T(8,128)(2,1)}, u32[]{:S(2)}, u32[]{:S(2)}) %all-to-all-start.2) | async-done | bytes 1572896 | tf_op jit(solution)/shard_map/all_to_all | solution.py:437
  76.6 4.7 %all-to-all-start = ((bf16[128,8,768]{2,1,0:T(8,128)(2,1)}), bf16[128,8,768]{2,1,0:T(8,128)(2,1)S(1)}, u32[]{:S(2)}, u32[]{:S(2)}) async-start(bf16[128,8,768]{2,1,0:T(8,128)(2,1)} %get-tuple-element.25), calls=%async_computation | async-start | bytes 3145728 | tf_op jit(solution)/shard_map/all_to_all | solution.py:437
  81.3 14.3 %expert.3 = bf16[128,8,768]{2,1,0:T(8,128)(2,1)} custom-call(bf16[128,8,768]{2,1,0:T(8,128)(2,1)} %all-to-all-done.2.x_ref, bf16[1,768,3072]{2,1,0:T(8,128)(2,1)} %in_ref.3, bf16[1,3072,768]{2,1,0:T(8,128)(2,1)} %out_ref.3), custom_call_target="tpu_custom_call" | custom-call | tf_op jit(solution)/shard_map/expert/pallas_call | solution.py:443
  95.6 10.4 %all-to-all-done.x_ref = bf16[128,8,768]{2,1,0:T(8,128)(2,1)S(1)} async-done(((bf16[128,8,768]{2,1,0:T(8,128)(2,1)}), bf16[128,8,768]{2,1,0:T(8,128)(2,1)S(1)}, u32[]{:S(2)}, u32[]{:S(2)}) %all-to-all-start) | async-done | bytes 1572896 | tf_op jit(solution)/shard_map/all_to_all | solution.py:437
  106.0 4.7 %all-to-all-start.3 = ((bf16[128,8,768]{2,1,0:T(8,128)(2,1)}), bf16[128,8,768]{2,1,0:T(8,128)(2,1)S(1)}, u32[]{:S(2)}, u32[]{:S(2)}) async-start(bf16[128,8,768]{2,1,0:T(8,128)(2,1)} %expert.3), calls=%async_computation.3 | async-start | bytes 3145728 | tf_op jit(solution)/shard_map/all_to_all | solution.py:437
  110.7 13.8 %expert.2 = bf16[128,8,768]{2,1,0:T(8,128)(2,1)} custom-call(bf16[128,8,768]{2,1,0:T(8,128)(2,1)S(1)} %all-to-all-done.x_ref, bf16[1,768,3072]{2,1,0:T(8,128)(2,1)} %in_ref.3, bf16[1,3072,768]{2,1,0:T(8,128)(2,1)} %out_ref.3), custom_call_target="tpu_custom_call" | custom-call | tf_op jit(solution)/shard_map/expert/pallas_call | solution.py:443
  124.5 10.9 %all-to-all-done.3.back_ref = bf16[128,8,768]{2,1,0:T(8,128)(2,1)S(1)} async-done(((bf16[128,8,768]{2,1,0:T(8,128)(2,1)}), bf16[128,8,768]{2,1,0:T(8,128)(2,1)S(1)}, u32[]{:S(2)}, u32[]{:S(2)}) %all-to-all-start.3) | async-done | bytes 1572896 | tf_op jit(solution)/shard_map/all_to_all | solution.py:437
  135.4 4.7 %all-to-all-start.1 = ((bf16[128,8,768]{2,1,0:T(8,128)(2,1)}), bf16[128,8,768]{2,1,0:T(8,128)(2,1)S(1)}, u32[]{:S(2)}, u32[]{:S(2)}) async-start(bf16[128,8,768]{2,1,0:T(8,128)(2,1)} %expert.2), calls=%async_computation.1 | async-start | bytes 3145728 | tf_op jit(solution)/shard_map/all_to_all | solution.py:437
  140.1 3.1 %combine0.1.held_ref = bf16[2,512,768]{2,1,0:T(8,128)(2,1)} custom-call(bf16[512,768]{1,0:T(8,128)(2,1)} %get-tuple-element.28.att_ref, f32[512,128]{1,0:T(8,128)} %get-tuple-element.29.aux_ref, bf16[128,8,768]{2,1,0:T(8,128)(2,1)S(1)} %all-to-all-done.3.back_ref), custom_call_target="tpu_custom_call" | custom-call | tf_op jit(solution)/shard_map/combine0/pallas_call | solution.py:468
  143.2 21.6 %all-to-all-done.1.back_ref = bf16[128,8,768]{2,1,0:T(8,128)(2,1)S(1)} async-done(((bf16[128,8,768]{2,1,0:T(8,128)(2,1)}), bf16[128,8,768]{2,1,0:T(8,128)(2,1)S(1)}, u32[]{:S(2)}, u32[]{:S(2)}) %all-to-all-start.1) | async-done | bytes 1572896 | tf_op jit(solution)/shard_map/all_to_all | solution.py:437
  164.8 3.1 %combine1.1 = bf16[2,512,768]{2,1,0:T(8,128)(2,1)} custom-call(bf16[512,768]{1,0:T(8,128)(2,1)} %get-tuple-element.23.att_ref, f32[512,128]{1,0:T(8,128)} %get-tuple-element.24.aux_ref, bf16[128,8,768]{2,1,0:T(8,128)(2,1)S(1)} %all-to-all-done.1.back_ref, bf16[2,512,768]{2,1,0:T(8,128)(2,1)} %combine0.1.held_ref), custom_call_target="tpu_custom_call", output_to_operand_aliasing={{}: (3, {})} | custom-call | tf_op jit(solution)/shard_map/combine1/pallas_call | solution.py:477
  (20 shorter events, 0.5 us)
Async XLA Ops:
  1.0 9.6 %collective-permute-start = (bf16[48,1536]{1,0:T(8,128)(2,1)S(1)}, bf16[48,1536]{1,0:T(8,128)(2,1)S(1)}, u32[]{:S(2)}, u32[]{:S(2)}) collective-permute-start(bf16[48,1536]{1,0:T(8,128)(2,1)S(1)} %maximum_select_fusion), channel_id=1, source_target_pairs={{0,32},{1,9},{2,34},{3,11},{4,36},{5,13},{6,38},{7,15},{8,40},{9,1... | collective-permute-start | bytes 442376 | tf_op jit(solution)/shard_map/ppermute | solution.py:333
  3.5 7.1 %collective-permute-start.1 = (bf16[48,1536]{1,0:T(8,128)(2,1)S(1)}, bf16[48,1536]{1,0:T(8,128)(2,1)S(1)}, u32[]{:S(2)}, u32[]{:S(2)}) collective-permute-start(bf16[48,1536]{1,0:T(8,128)(2,1)S(1)} %maximum_select_fusion), channel_id=1, source_target_pairs={{0,96},{1,25},{2,98},{3,27},{4,100},{5,29},{6,102},{7,31},{8,104},... | collective-permute-start | bytes 442376 | tf_op jit(solution)/shard_map/ppermute | solution.py:333
  5.7 5.8 %collective-permute-start.2 = (bf16[48,1536]{1,0:T(8,128)(2,1)S(1)}, bf16[48,1536]{1,0:T(8,128)(2,1)S(1)}, u32[]{:S(2)}, u32[]{:S(2)}) collective-permute-start(bf16[48,1536]{1,0:T(8,128)(2,1)S(1)} %maximum_select_fusion), channel_id=1, source_target_pairs={{0,64},{1,17},{2,66},{3,19},{4,68},{5,21},{6,70},{7,23},{8,72},{9,... | collective-permute-start | bytes 442376 | tf_op jit(solution)/shard_map/ppermute | solution.py:333
  6.9 1.4 copy-start
  8.3 0.7 copy-start.4
  9.0 0.7 copy-start.6
  10.5 16.9 %copy-start.5 = (s32[2,1,512]{2,1,0:T(1,128)}, s32[2,1,512]{2,1,0:T(1,128)S(1)}, u32[]{:S(2)}) copy-start(s32[2,1,512]{2,1,0:T(1,128)S(1)} %get-tuple-element.22.position_ref) | copy-start | bytes 12292
  10.6 22.1 %copy-start.3 = (bf16[2,512,768]{2,1,0:T(8,128)(2,1)}, bf16[2,512,768]{2,1,0:T(8,128)(2,1)S(1)}, u32[]{:S(2)}) copy-start(bf16[2,512,768]{2,1,0:T(8,128)(2,1)S(1)} %get-tuple-element.20.n_ref) | copy-start | bytes 4718596
  11.5 10.3 %collective-permute-start.3 = (bf16[192,1536]{1,0:T(8,128)(2,1)S(1)}, bf16[192,1536]{1,0:T(8,128)(2,1)S(1)}, u32[]{:S(2)}, u32[]{:S(2)}) collective-permute-start(bf16[192,1536]{1,0:T(8,128)(2,1)S(1)} %pad_maximum_fusion.m0.b0), channel_id=1, source_target_pairs={{0,8},{1,33},{2,10},{3,35},{4,12},{5,37},{6,14},{7,39},{8,16},{9,4... | collective-permute-start | bytes 1769480 | tf_op jit(solution)/shard_map/ppermute | solution.py:355
  12.5 14.9 %collective-permute-start.4 = (bf16[192,1536]{1,0:T(8,128)(2,1)S(1)}, bf16[192,1536]{1,0:T(8,128)(2,1)S(1)}, u32[]{:S(2)}, u32[]{:S(2)}) collective-permute-start(bf16[192,1536]{1,0:T(8,128)(2,1)S(1)} %pad_maximum_fusion.m0.b0), channel_id=1, source_target_pairs={{0,24},{1,97},{2,26},{3,99},{4,28},{5,101},{6,30},{7,103},{8,0},{9... | collective-permute-start | bytes 1769480 | tf_op jit(solution)/shard_map/ppermute | solution.py:355
  14.3 14.6 %collective-permute-start.5 = (bf16[192,1536]{1,0:T(8,128)(2,1)S(1)}, bf16[192,1536]{1,0:T(8,128)(2,1)S(1)}, u32[]{:S(2)}, u32[]{:S(2)}) collective-permute-start(bf16[192,1536]{1,0:T(8,128)(2,1)S(1)} %pad_maximum_fusion.m0.b0), channel_id=1, source_target_pairs={{0,16},{1,65},{2,18},{3,67},{4,20},{5,69},{6,22},{7,71},{8,24},{9,... | collective-permute-start | bytes 1769480 | tf_op jit(solution)/shard_map/ppermute | solution.py:355
  28.9 7.9 %collective-permute-start.7 = (bf16[576,1536]{1,0:T(8,128)(2,1)S(1)}, bf16[576,1536]{1,0:T(8,128)(2,1)S(1)}, u32[]{:S(2)}, u32[]{:S(2)}) collective-permute-start(bf16[576,1536]{1,0:T(8,128)(2,1)S(1)} %constant_dynamic-update-slice_fusion.m1.b1), channel_id=1, source_target_pairs={{0,1},{1,0},{2,3},{3,2},{4,5},{5,4},{6,7},{7,6},{8,9},{9,8},{10,11... | collective-permute-start | bytes 5308424 | tf_op jit(solution)/shard_map/ppermute | solution.py:357
  32.3 4.4 %collective-permute-start.6 = (bf16[192,1536]{1,0:T(8,128)(2,1)S(1)}, bf16[192,1536]{1,0:T(8,128)(2,1)S(1)}, u32[]{:S(2)}, u32[]{:S(2)}) collective-permute-start(bf16[192,1536]{1,0:T(8,128)(2,1)S(1)} %pad_maximum_fusion.m0.b0), channel_id=1, source_target_pairs={{0,1},{1,0},{2,3},{3,2},{4,5},{5,4},{6,7},{7,6},{8,9},{9,8},{10,11... | collective-permute-start | bytes 1769480 | tf_op jit(solution)/shard_map/ppermute | solution.py:357
  36.8 8.2 %copy-start.1 = (bf16[576,1536]{1,0:T(8,128)(2,1)}, bf16[576,1536]{1,0:T(8,128)(2,1)S(1)}, u32[]{:S(2)}) copy-start(bf16[576,1536]{1,0:T(8,128)(2,1)S(1)} %collective-permute-done.7.o1) | copy-start | bytes 5308420
  45.0 31.6 %all-to-all-start.2 = ((bf16[128,8,768]{2,1,0:T(8,128)(2,1)}), bf16[128,8,768]{2,1,0:T(8,128)(2,1)}, u32[]{:S(2)}, u32[]{:S(2)}) async-start(bf16[128,8,768]{2,1,0:T(8,128)(2,1)} %get-tuple-element.30), calls=%async_computation.2 | async-start | bytes 3145728 | tf_op jit(solution)/shard_map/all_to_all | solution.py:437
  52.3 1.5 copy-start.2
  76.6 29.4 %all-to-all-start = ((bf16[128,8,768]{2,1,0:T(8,128)(2,1)}), bf16[128,8,768]{2,1,0:T(8,128)(2,1)S(1)}, u32[]{:S(2)}, u32[]{:S(2)}) async-start(bf16[128,8,768]{2,1,0:T(8,128)(2,1)} %get-tuple-element.25), calls=%async_computation | async-start | bytes 3145728 | tf_op jit(solution)/shard_map/all_to_all | solution.py:437
  106.0 29.4 %all-to-all-start.3 = ((bf16[128,8,768]{2,1,0:T(8,128)(2,1)}), bf16[128,8,768]{2,1,0:T(8,128)(2,1)S(1)}, u32[]{:S(2)}, u32[]{:S(2)}) async-start(bf16[128,8,768]{2,1,0:T(8,128)(2,1)} %expert.3), calls=%async_computation.3 | async-start | bytes 3145728 | tf_op jit(solution)/shard_map/all_to_all | solution.py:437
  135.4 29.4 %all-to-all-start.1 = ((bf16[128,8,768]{2,1,0:T(8,128)(2,1)}), bf16[128,8,768]{2,1,0:T(8,128)(2,1)S(1)}, u32[]{:S(2)}, u32[]{:S(2)}) async-start(bf16[128,8,768]{2,1,0:T(8,128)(2,1)} %expert.2), calls=%async_computation.1 | async-start | bytes 3145728 | tf_op jit(solution)/shard_map/all_to_all | solution.py:437
